TPU v7x, 32 devices: a whole 2x2x4 slice. The times are simulated.
32 devices in a mesh: groups: 2 (over y), store: 16 (over z, x, core).
Axes of the slice: x: 2, y: 2, z: 4, core: 2. Of those that a mesh axis runs over, the one named last changes fastest.
Arguments:
- queries: bfloat16 [2, 32, 8192], P(None, ('groups', 'store')), parts along dimension 1, may hold values from -6 to 206
- new_keys: bfloat16 [2, 32, 1024], P(None, ('groups', 'store')), parts along dimension 1, may hold values from -6 to 12.5
- incoming_values: bfloat16 [2, 32, 1024], P(None, ('groups', 'store')), parts along dimension 1, may hold values from -6 to 6
- key_left: bfloat16 [32, 4096, 160], P(('groups', 'store')), parts along dimension 0, may hold values from -12 to 12
- right_key_factor: bfloat16 [32, 160, 1024], P(('groups', 'store')), parts along dimension 0, may hold values from -0.5 to 0.5
- value_tile_store: bfloat16 [131072, 1024], P(('groups', 'store')), parts along dimension 0, may hold values from -6 to 6
- slot_map: int32 [32, 8, 512], P(('groups', 'store')), parts along dimension 0, may hold values from 0 to 65535, as said below
- chosen: int32 [2, 32, 8, 64], P(None, ('groups', 'store')), parts along dimension 1, may hold values from 0 to 511, as said below
- lengths: int32 [32], P(('groups', 'store')), parts along dimension 0, may hold values from 1024 to 4096
Outputs:
- attended: bfloat16 [2, 32, 8192], P(None, ('groups', 'store')), parts along dimension 1
There are 2 independent parts, one for each index of `groups`. A program takes and returns all parts, laid end to end along the dimension named above; each array names one. Nothing has to cross between parts.
Inputs may be any that keep to these rules, and one draw needn't show every extreme that they name: `slot_map`: the entries are distinct; pool rows r * 4096 to (r+1) * 4096 - 1 stand on index r of store. `chosen`: the 64 blocks of one step, request and key head are distinct; at most 8 of them have their slot_map row on one index of store, and in every step some index of store holds exactly 8 of them for every request and key head.
All inputs are finite; a program needn't handle non-finite values.
Results may differ from a plain program's by a relative error of at most 0.005.
The roundings to bfloat16 on the way count: a program that leaves them out, or rounds other values in their place, can miss the bound.
Values may be sent and summed in bfloat16 or wider, within the bound.
A program may use at most 64 MiB of HBM per device.

v0:
```python
import jax
import jax.numpy as jnp
from jax import lax
from jax.sharding import PartitionSpec as P

KEY_VALUE_HEADS = 8
HEAD_SIZE = 128
BLOCK_TOKENS = 8


ROPE_BASE = 500000.0


def apply_rotary(tensor, token_positions):
    half_dim = tensor.shape[-1] // 2
    inverse = ROPE_BASE ** (-(jnp.arange(half_dim, dtype=jnp.float32) * 2.0 / tensor.shape[-1]))
    angles = jnp.asarray(token_positions).astype(jnp.float32)[..., None] * inverse
    cosine = jnp.cos(angles)
    sine_vals = jnp.sin(angles)
    first_half = tensor[..., :half_dim]
    second_half = tensor[..., half_dim:]
    return jnp.concatenate(
        [
            first_half * cosine - second_half * sine_vals,
            second_half * cosine + first_half * sine_vals,
        ],
        -1,
    )


def fetch_tiles(requests, value_tile_store):
    tile_row_index = jnp.take(
        value_tile_store,
        lax.all_to_all(requests, "store", split_axis=0, concat_axis=0, tiled=True),
        axis=0,
    )
    return lax.all_to_all(tile_row_index, "store", split_axis=0, concat_axis=0, tiled=True)


def build_requests(flat_idx, inside, total):
    buffer = jnp.zeros((total,), jnp.int32)
    return buffer.at[flat_idx.reshape(-1)].set(inside.reshape(-1))


def attend_row(
    query_full,
    incoming_keys_full,
    incoming_values_full,
    left_rows,
    right_factor_rows,
    block_numbers,
    tile_row_index,
    length,
    step_index,
):
    query_group_size = query_full.shape[-1] // HEAD_SIZE // KEY_VALUE_HEADS
    every_head = query_group_size * KEY_VALUE_HEADS
    selected_count = block_numbers.shape[1]
    score_scale = HEAD_SIZE ** (-0.5)
    right_factor_heads = right_factor_rows.reshape(
        right_factor_rows.shape[0], KEY_VALUE_HEADS, HEAD_SIZE
    )
    token_positions = (
        block_numbers[:, :, None] * BLOCK_TOKENS + jnp.arange(BLOCK_TOKENS, dtype=jnp.int32)
    ).reshape(KEY_VALUE_HEADS, selected_count * BLOCK_TOKENS)
    picked = left_rows[token_positions]
    raw_keys = jnp.einsum(
        "htr,rhd->htd", picked, right_factor_heads, preferred_element_type=jnp.float32
    )
    cache_keys = apply_rotary(raw_keys, token_positions).astype(jnp.bfloat16)
    rotated_query = apply_rotary(
        query_full[step_index].reshape(every_head, HEAD_SIZE).astype(jnp.float32),
        length + step_index,
    ).astype(jnp.bfloat16)
    current_position = (length + jnp.arange(step_index + 1, dtype=jnp.int32))[:, None]
    current_keys = apply_rotary(
        incoming_keys_full[: step_index + 1]
        .reshape(step_index + 1, KEY_VALUE_HEADS, HEAD_SIZE)
        .astype(jnp.float32),
        current_position,
    ).astype(jnp.bfloat16)
    current_keys = jnp.transpose(current_keys, (1, 0, 2))
    current_values = jnp.transpose(
        incoming_values_full[: step_index + 1].reshape(step_index + 1, KEY_VALUE_HEADS, HEAD_SIZE),
        (1, 0, 2),
    )
    local_values = tile_row_index.reshape(KEY_VALUE_HEADS, selected_count * BLOCK_TOKENS, HEAD_SIZE)
    grouped_queries = rotated_query.reshape(KEY_VALUE_HEADS, query_group_size, HEAD_SIZE)
    cache_scores = (
        jnp.einsum("hgd,htd->hgt", grouped_queries, cache_keys, preferred_element_type=jnp.float32)
        * score_scale
    )
    inside_len = token_positions < length
    cache_scores = jnp.where(inside_len[:, None, :], cache_scores, -jnp.inf)
    fresh_scores = (
        jnp.einsum(
            "hgd,hnd->hgn", grouped_queries, current_keys, preferred_element_type=jnp.float32
        )
        * score_scale
    )
    highest = jnp.maximum(
        jnp.max(cache_scores, -1, keepdims=True), jnp.max(fresh_scores, -1, keepdims=True)
    )
    cache_exp = jnp.exp(cache_scores - highest)
    fresh_exp = jnp.exp(fresh_scores - highest)
    denominator = jnp.sum(cache_exp, -1, keepdims=True) + jnp.sum(fresh_exp, -1, keepdims=True)
    cache_weight = (cache_exp / denominator).astype(jnp.bfloat16)
    fresh_weight = (fresh_exp / denominator).astype(jnp.bfloat16)
    attended = jnp.einsum(
        "hgt,htd->hgd", cache_weight, local_values, preferred_element_type=jnp.float32
    )
    attended = attended + jnp.einsum(
        "hgn,hnd->hgd", fresh_weight, current_values, preferred_element_type=jnp.float32
    )
    return attended.reshape(every_head * HEAD_SIZE).astype(jnp.bfloat16)


def per_device(
    queries,
    new_keys,
    incoming_values,
    key_left,
    right_key_factor,
    value_tile_store,
    slot_map,
    chosen,
    lengths,
):
    nstore = lax.axis_size("store")
    local_rows = key_left.shape[0]
    nchunk = slot_map.shape[2]
    step_count = chosen.shape[0]
    selected_count = chosen.shape[3]
    keeper_share = max(1, nchunk // nstore // 4)
    tile_limit = local_rows * KEY_VALUE_HEADS * keeper_share
    pool_here = value_tile_store.shape[0]
    slot_numbers = jnp.take_along_axis(
        jnp.broadcast_to(slot_map[None], (step_count,) + slot_map.shape), chosen, axis=3
    )
    tile_keeper = slot_numbers // pool_here
    inside = slot_numbers % pool_here
    matched = tile_keeper[..., :, None] == tile_keeper[..., None, :]
    earlier = jnp.arange(selected_count)[None, :] < jnp.arange(selected_count)[:, None]
    order_in = jnp.sum(jnp.logical_and(matched, earlier), -1)
    row_head = (
        jnp.arange(local_rows, dtype=jnp.int32)[:, None, None] * KEY_VALUE_HEADS
        + jnp.arange(KEY_VALUE_HEADS, dtype=jnp.int32)[None, :, None]
    )
    position = row_head * keeper_share + order_in
    tiles_all = []
    slot_span = step_count * tile_limit
    flat_idx = (
        tile_keeper * slot_span
        + jnp.arange(step_count, dtype=jnp.int32)[:, None, None, None] * tile_limit
        + position
    )
    requests = build_requests(flat_idx, inside, nstore * slot_span).reshape(nstore, slot_span)
    received = fetch_tiles(requests, value_tile_store).reshape(nstore * slot_span, -1)
    for step_index in range(step_count):
        tiles_all.append(received[flat_idx[step_index]])
    results = []
    for step_index in range(step_count):
        per_rows = [
            attend_row(
                queries[:, 0],
                new_keys[:, 0],
                incoming_values[:, 0],
                key_left[0],
                right_key_factor[0],
                chosen[step_index, 0],
                tiles_all[step_index][0],
                lengths[0],
                step_index,
            )
        ]
        results.append(jnp.stack(per_rows))
    return jnp.stack(results)


def solution(mesh):
    in_specs = (
        P(None, ("groups", "store"), None),
        P(None, ("groups", "store"), None),
        P(None, ("groups", "store"), None),
        P(("groups", "store"), None, None),
        P(("groups", "store"), None, None),
        P(("groups", "store"), None),
        P(("groups", "store"), None, None),
        P(None, ("groups", "store"), None, None),
        P(("groups", "store")),
    )
    out_specs = P(None, ("groups", "store"), None)
    return jax.shard_map(
        per_device, mesh=mesh, in_specs=in_specs, out_specs=out_specs, check_vma=False
    )
```

profile of v0, /device:TPU:11, one launch (start us, length us, event | category | flops | bytes accessed | tf_op | source)
XLA Modules:
  0.0 157.6 jit_solution(14860396995195361211)
XLA Ops:
  0.0 0.7 bitcast_or_fusion
  0.7 0.1 reshape.724
  0.8 8.4 %gather_fusion.5 = s32[1024]{0:T(1024)S(1)} fusion(s32[2,8,512]{2,1,0:T(8,128)S(1)} %broadcast.481, s32[1024]{0:T(1024)S(1)} %reshape.724), kind=kCustom, calls=%fused_computation.5 | custom fusion | bytes 20480 | tf_op jit(solution)/shard_map/jit(take_along_axis)/gather | solution.py:137
  9.4 0.5 convert_reduce_fusion
  9.9 0.1 fusion.45
  10.0 0.1 reshape.673
  10.1 4.9 %scatter_custom_fusion = s32[2048]{0:T(1024)} fusion(s32[1024]{0:T(1024)S(1)} %bitcast.150, s32[1024]{0:T(1024)S(1)} %reshape.734, s32[]{:T(128)} %constant.79.clone.1), kind=kCustom, calls=%fused_computation.123 | custom fusion | bytes 8196 | tf_op jit(solution)/shard_map/scatter | solution.py:42
  14.9 6.5 %all-to-all-start = ((s32[16,1,128]{2,1,0:T(1,128)}), s32[16,1,128]{2,1,0:T(1,128)S(1)}, u32[]{:S(2)}, u32[]{:S(2)}) async-start(s32[16,1,128]{2,1,0:T(1,128)} %bitcast.22), calls=%async_computation | async-start | bytes 16384 | tf_op jit(solution)/shard_map/all_to_all | solution.py:34
  21.5 0.1 add.272
  21.6 0.1 add.269
  21.7 0.2 add.276
  21.9 0.1 add.299
  22.0 0.2 add.304
  22.2 3.0 %all-to-all-done = s32[16,1,128]{2,1,0:T(1,128)S(1)} async-done(((s32[16,1,128]{2,1,0:T(1,128)}), s32[16,1,128]{2,1,0:T(1,128)S(1)}, u32[]{:S(2)}, u32[]{:S(2)}) %all-to-all-start) | async-done | bytes 8224 | tf_op jit(solution)/shard_map/all_to_all | solution.py:34
  25.3 15.4 %gather_fusion.1 = bf16[2048,1024]{1,0:T(8,128)(2,1)} fusion(bf16[4096,1024]{1,0:T(8,128)(2,1)} %param.14, s32[2048]{0:T(1024)S(1)} %fusion.44), kind=kCustom, calls=%fused_computation.1 | custom fusion | bytes 8396800 | tf_op jit(solution)/shard_map/jit(_take)/gather | solution.py:32
  40.7 3.8 %broadcast_select_fusion = bf16[16,128,1024]{2,1,0:T(8,128)(2,1)} fusion(bf16[16,128,1024]{2,1,0:T(8,128)(2,1)} %bitcast.131, pred[16,128]{1,0:T(8,128)(4,1)S(1)} %compare_and_fusion), kind=kLoop, calls=%fused_computation.7 | loop fusion | flops 2097152 | bytes 8390656 | tf_op jit(solution)/shard_map/jit(_take)/select_n | solution.py:32
  44.5 7.1 %all-to-all-start.1 = ((bf16[16,128,1024]{2,1,0:T(8,128)(2,1)}), bf16[16,128,1024]{2,1,0:T(8,128)(2,1)}, u32[]{:S(2)}, u32[]{:S(2)}) async-start(bf16[16,128,1024]{2,1,0:T(8,128)(2,1)} %broadcast_select_fusion), calls=%async_computation.1 | async-start | bytes 8388608 | tf_op jit(solution)/shard_map/all_to_all | solution.py:37
  51.6 0.2 add.270
  51.8 0.2 add.300
  52.6 0.1 reshape.700
  52.7 0.1 reshape.716
  52.8 3.1 %copy.40 = bf16[1,4096,160]{2,1,0:T(8,128)(2,1)S(1)} copy(bf16[1,4096,160]{1,2,0:T(8,128)(2,1)} %param.12) | data formatting | bytes 2621440 | tf_op args[3]
  55.9 16.9 %gather_fusion.3 = bf16[4096,160]{1,0:T(8,128)(2,1)} fusion(bf16[4096,160]{1,0:T(8,128)(2,1)S(1)} %bitcast.129, s32[4096]{0:T(1024)S(1)} %broadcast_clamp_fusion), kind=kCustom, calls=%fused_computation.3 | custom fusion | bytes 2637824 | tf_op jit(solution)/shard_map/gather | solution.py:66
  72.9 16.9 %gather_fusion = bf16[4096,160]{1,0:T(8,128)(2,1)} fusion(bf16[4096,160]{1,0:T(8,128)(2,1)S(1)} %bitcast.130, s32[4096]{0:T(1024)S(1)} %broadcast_clamp_fusion.1), kind=kCustom, calls=%fused_computation | custom fusion | bytes 2637824 | tf_op jit(solution)/shard_map/gather | solution.py:66
  89.9 0.1 multiply_cosine_fusion.2
  90.0 0.1 subtract_convert_fusion.2
  90.2 0.1 fusion.39
  90.2 0.2 fusion.68
  90.5 2.6 %fusion.28 = f32[8,512,128]{1,2,0:T(8,128)S(1)} fusion(bf16[8,512,160]{2,1,0:T(8,128)(2,1)} %bitcast.133, bf16[160,8,128]{2,1,0:T(8,128)(2,1)S(1)} %bitcast.134), kind=kOutput, calls=%fused_computation.46 | convolution fusion | flops 167772160 | bytes 3735552 | tf_op jit(solution)/shard_map/htr,rhd->htd/dot_general | solution.py:67
  93.1 0.8 fusion.26
  93.9 8.2 %fusion.17 = (bf16[8,512,64]{1,2,0:T(8,128)(2,1)S(1)}, bf16[8,512,64]{1,2,0:T(8,128)(2,1)S(1)}, bf16[8,512,64]{1,2,0:T(8,128)(2,1)S(1)}, bf16[8,512,64]{1,2,0:T(8,128)(2,1)S(1)}) fusion(f32[8,512,128]{1,2,0:T(8,128)S(1)} %fusion.28, f32[64]{0:T(128)S(1)} %negate_power_fusion, f32[8,512]{1,0:T(8,128)S(1)} %get-tuple-element.27, ...), kind=kLoop, calls=%fused_computation.34 | loop fusion | flops 4718592 | bytes 6324480 | tf_op jit(solution)/shard_map/convert.20
  102.1 0.4 fusion.67
  102.5 0.2 fusion.31
  102.8 0.1 fusion.58
  102.9 0.1 maximum_bitcast_fusion.2
  103.0 0.1 fusion.37
  103.1 0.2 fusion.56
  103.3 0.4 fusion.69
  103.7 0.2 fusion.30
  103.9 40.2 %all-to-all-done.1 = bf16[16,128,1024]{2,1,0:T(8,128)(2,1)} async-done(((bf16[16,128,1024]{2,1,0:T(8,128)(2,1)}), bf16[16,128,1024]{2,1,0:T(8,128)(2,1)}, u32[]{:S(2)}, u32[]{:S(2)}) %all-to-all-start.1) | async-done | bytes 4194336 | tf_op jit(solution)/shard_map/all_to_all | solution.py:37
  144.1 5.5 %gather_fusion.4 = bf16[512,1024]{1,0:T(8,128)(2,1)S(1)} fusion(bf16[2048,1024]{1,0:T(8,128)(2,1)} %bitcast.27, s32[1024]{0:T(1024)S(1)} %pad_clamp_fusion), kind=kCustom, calls=%fused_computation.4 | custom fusion | bytes 2099200 | tf_op jit(solution)/shard_map/gather | solution.py:160
  149.6 5.5 %gather_fusion.2 = bf16[512,1024]{1,0:T(8,128)(2,1)S(1)} fusion(bf16[2048,1024]{1,0:T(8,128)(2,1)} %bitcast.27, s32[1024]{0:T(1024)S(1)} %pad_clamp_fusion.1), kind=kCustom, calls=%fused_computation.2 | custom fusion | bytes 2099200 | tf_op jit(solution)/shard_map/gather | solution.py:160
  155.0 0.5 reshape_squeeze.17
  155.6 0.5 reshape_squeeze.18
  156.1 0.3 fusion.32
  156.3 0.2 fusion.11
  156.6 0.3 fusion.10
  156.9 0.7 pad_maximum_fusion
  (54 shorter events, 0.7 us)
Async XLA Ops:
  0.0 0.8 copy-start
  0.8 8.5 %copy-start.4 = (s32[2,1,8,64]{3,2,1,0:T(8,128)S(1)}, s32[2,1,8,64]{3,2,1,0:T(8,128)}, u32[]{:S(2)}) copy-start(s32[2,1,8,64]{3,2,1,0:T(8,128)} %param.16) | copy-start | bytes 12292
  14.9 10.3 %all-to-all-start = ((s32[16,1,128]{2,1,0:T(1,128)}), s32[16,1,128]{2,1,0:T(1,128)S(1)}, u32[]{:S(2)}, u32[]{:S(2)}) async-start(s32[16,1,128]{2,1,0:T(1,128)} %bitcast.22), calls=%async_computation | async-start | bytes 16384 | tf_op jit(solution)/shard_map/all_to_all | solution.py:34
  44.5 8.3 %copy-start.2 = (bf16[1,160,1024]{2,1,0:T(8,128)(2,1)S(1)}, bf16[1,160,1024]{2,1,0:T(8,128)(2,1)}, u32[]{:S(2)}) copy-start(bf16[1,160,1024]{2,1,0:T(8,128)(2,1)} %param.13) | copy-start | bytes 983044
  44.5 99.6 %all-to-all-start.1 = ((bf16[16,128,1024]{2,1,0:T(8,128)(2,1)}), bf16[16,128,1024]{2,1,0:T(8,128)(2,1)}, u32[]{:S(2)}, u32[]{:S(2)}) async-start(bf16[16,128,1024]{2,1,0:T(8,128)(2,1)} %broadcast_select_fusion), calls=%async_computation.1 | async-start | bytes 8388608 | tf_op jit(solution)/shard_map/all_to_all | solution.py:37
  72.9 17.1 %copy-start.5 = (bf16[2,1,1024]{2,0,1:T(2,128)(2,1)S(1)}, bf16[2,1,1024]{2,0,1:T(2,128)(2,1)}, u32[]{:S(2)}) copy-start(bf16[2,1,1024]{2,0,1:T(2,128)(2,1)} %param.10) | copy-start | bytes 12292
  72.9 17.2 %copy-start.3 = (bf16[2,1,8192]{2,0,1:T(2,128)(2,1)S(1)}, bf16[2,1,8192]{2,0,1:T(2,128)(2,1)}, u32[]{:S(2)}) copy-start(bf16[2,1,8192]{2,0,1:T(2,128)(2,1)} %param.9) | copy-start | bytes 98308
  90.5 2.6 %copy-start.1 = (bf16[4096,160]{1,0:T(8,128)(2,1)S(1)}, bf16[4096,160]{1,0:T(8,128)(2,1)}, u32[]{:S(2)}) copy-start(bf16[4096,160]{1,0:T(8,128)(2,1)} %gather_fusion.3) | copy-start | bytes 3932164
  102.1 1.8 %copy-start.6 = (bf16[2,1,1024]{2,0,1:T(2,128)(2,1)S(1)}, bf16[2,1,1024]{2,0,1:T(2,128)(2,1)}, u32[]{:S(2)}) copy-start(bf16[2,1,1024]{2,0,1:T(2,128)(2,1)} %param.11) | copy-start | bytes 12292
where the time goes:
time: 158 us
  local copies, waits for them, and re-layouts  79.1 us (50%)
  waiting for transfers between devices  43.2 us (27%)
  other arithmetic  15.2 us (10%)
  starting transfers between devices  13.6 us (9%)
  matrix products  5.36 us (3%)
    all_to_all x1, waiting for transfers between devices, fetch_tiles(): lax.all_to_all(tile_row_index, 'store', split_axis=0, concat_axis=0, tile...  40.2 us
    gather x2, local copies, waits for them, and re-layouts, attend_row(): picked = left_rows[token_positions]  33.8 us
    gather x1, local copies, waits for them, and re-layouts, fetch_tiles(): jnp.take(value_tile_store, lax.all_to_all(requests, 'store', split_axis=0...  15.4 us
    gather x2, local copies, waits for them, and re-layouts, per_device(): tiles_all.append(received[flat_idx[step_index]])  10.9 us
    gather x3, local copies, waits for them, and re-layouts, per_device(): jnp.take_along_axis(jnp.broadcast_to(slot_map[None], (step_count,) + slot...  8.53 us
    another operation x4, other arithmetic  8.28 us
    all_to_all x1, starting transfers between devices, fetch_tiles(): lax.all_to_all(tile_row_index, 'store', split_axis=0, concat_axis=0, tile...  7.11 us
    all_to_all x1, starting transfers between devices, fetch_tiles(): lax.all_to_all(requests, 'store', split_axis=0, concat_axis=0, tiled=True)  6.52 us
  transfers between devices with their start and end apart: 2, of which 2 were waited for; matrix products, arithmetic and copies ran while one was open for 33% of the time, Pallas kernels for 0%

commit v1 on v0

--- a/solution.py
+++ b/solution.py
@@ -1,6 +1,10 @@
+import functools
+
 import jax
 import jax.numpy as jnp
 from jax import lax
+from jax.experimental import pallas as pl
+from jax.experimental.pallas import tpu as pltpu
 from jax.sharding import PartitionSpec as P
 
 KEY_VALUE_HEADS = 8
@@ -177,6 +181,275 @@
     return jnp.stack(results)
 
 
+def plan_kernel(share, chosen_ref, keeper_ref, inside_ref, place_ref, request_ref):
+    rows, picks = chosen_ref.shape
+    heads, blocks = keeper_ref.shape
+    total = request_ref.shape[1]
+    holders = total // share
+    block_at = lax.broadcasted_iota(jnp.int32, (rows, blocks), 1)
+    chosen = chosen_ref[...]
+    hit = jnp.zeros((rows, blocks), jnp.int32)
+    for pick in range(picks):
+        hit = jnp.where(chosen[:, pick : pick + 1] == block_at, 1, hit)
+    keeper = jnp.concatenate([keeper_ref[...]] * (rows // heads), 0)
+    kept = jnp.where(hit == 1, keeper, -1)
+    before = (
+        lax.broadcasted_iota(jnp.int32, (blocks, blocks), 0)
+        < lax.broadcasted_iota(jnp.int32, (blocks, blocks), 1)
+    ).astype(jnp.float32).astype(jnp.bfloat16)
+    mine = [jnp.where(kept == holder, 1.0, 0.0) for holder in range(holders)]
+    counts = jnp.dot(
+        jnp.concatenate(mine, 0).astype(jnp.bfloat16), before, preferred_element_type=jnp.float32
+    )
+    order = jnp.zeros((rows, blocks), jnp.float32)
+    for holder in range(holders):
+        order = order + mine[holder] * counts[holder * rows : (holder + 1) * rows]
+    place = jnp.where(hit == 1, keeper * share + order.astype(jnp.int32), -1)
+    place_ref[...] = place
+    inside = inside_ref[...]
+    low = (inside & 255).astype(jnp.float32)
+    middle = ((inside >> 8) & 255).astype(jnp.float32)
+    high = (inside >> 16).astype(jnp.float32)
+    slot_at = lax.broadcasted_iota(jnp.int32, (total, blocks), 0)
+    for row in range(rows):
+        head = row % heads
+        digits = jnp.concatenate(
+            [low[head : head + 1], middle[head : head + 1], high[head : head + 1],
+             jnp.zeros((5, blocks), jnp.float32)], 0
+        ).astype(jnp.bfloat16)
+        table = jnp.where(place[row : row + 1] == slot_at, 1.0, 0.0).astype(jnp.bfloat16)
+        found = lax.dot_general(
+            digits, table, (((1,), (1,)), ((), ())), preferred_element_type=jnp.float32
+        ).astype(jnp.int32)
+        request_ref[row : row + 1, :] = found[0:1] + found[1:2] * 256 + found[2:3] * 65536
+
+
+def weigh_kernel(
+    share, length_ref, query_ref, fresh_key_ref, fresh_value_ref, left_ref, right_ref, place_ref,
+    coarse_cos_ref, coarse_sin_ref, fine_cos_ref, fine_sin_ref,
+    wire_ref, fresh_ref, cos_ref, sin_ref, sent_ref,
+):
+    head = pl.program_id(0)
+    heads = pl.num_programs(0)
+    in_block, blocks, _ = left_ref.shape
+    steps = place_ref.shape[1]
+    both = query_ref.shape[1]
+    group = both // steps
+    holders = wire_ref.shape[0]
+    length = length_ref[0]
+
+    @pl.when(head == 0)
+    def _():
+        coarse_cos = coarse_cos_ref[...][:, None, :]
+        coarse_sin = coarse_sin_ref[...][:, None, :]
+        sign = jnp.where(
+            lax.broadcasted_iota(jnp.int32, (1, 1, HEAD_SIZE), 2) < HEAD_SIZE // 2, -1.0, 1.0
+        )
+        for j in range(in_block):
+            fine_cos = fine_cos_ref[j][None]
+            fine_sin = fine_sin_ref[j][None]
+            cos_ref[j] = (coarse_cos * fine_cos - coarse_sin * fine_sin).reshape(blocks, HEAD_SIZE)
+            sin_ref[j] = ((coarse_sin * fine_cos + coarse_cos * fine_sin) * sign).reshape(
+                blocks, HEAD_SIZE
+            )
+
+    query = query_ref[0]
+    place = place_ref[0]
+    place_rows = jnp.concatenate(
+        [jnp.broadcast_to(place[s : s + 1], (group, blocks)) for s in range(steps)], 0
+    )
+    block_at = lax.broadcasted_iota(jnp.int32, (both, blocks), 1)
+    scale = HEAD_SIZE ** (-0.5)
+    scores = []
+    for j in range(in_block):
+        raw = jnp.dot(left_ref[j], right_ref[...], preferred_element_type=jnp.float32)
+        keys = (
+            raw * cos_ref[j] + pltpu.roll(raw, HEAD_SIZE // 2, 1) * sin_ref[j]
+        ).astype(jnp.bfloat16)
+        score = lax.dot_general(
+            query, keys, (((1,), (1,)), ((), ())), preferred_element_type=jnp.float32
+        ) * scale
+        keep = jnp.logical_and(place_rows >= 0, block_at * in_block + j < length)
+        scores.append(jnp.where(keep, score, -jnp.inf))
+    fresh = lax.dot_general(
+        query, fresh_key_ref[0], (((1,), (1,)), ((), ())), preferred_element_type=jnp.float32
+    ) * scale
+    fresh_keep = (
+        lax.broadcasted_iota(jnp.int32, fresh.shape, 1)
+        <= lax.broadcasted_iota(jnp.int32, fresh.shape, 0) // group
+    )
+    fresh = jnp.where(fresh_keep, fresh, -jnp.inf)
+    top = scores[0]
+    for j in range(1, in_block):
+        top = jnp.maximum(top, scores[j])
+    highest = jnp.maximum(
+        jnp.max(top, -1, keepdims=True), jnp.max(fresh, -1, keepdims=True)
+    )
+    powers = [jnp.exp(score - highest) for score in scores]
+    fresh_power = jnp.exp(fresh - highest)
+    total = powers[0]
+    for j in range(1, in_block):
+        total = total + powers[j]
+    denominator = jnp.sum(total, -1, keepdims=True) + jnp.sum(fresh_power, -1, keepdims=True)
+    weights = [power / denominator for power in powers]
+    fresh_weight = (fresh_power / denominator).astype(jnp.bfloat16)
+    fresh_ref[0] = jnp.dot(fresh_weight, fresh_value_ref[0], preferred_element_type=jnp.float32)
+    slot_at = lax.broadcasted_iota(jnp.int32, (holders * share, blocks), 0)
+    for s in range(steps):
+        table = jnp.where(place[s : s + 1] == slot_at, 1.0, 0.0).astype(jnp.bfloat16)
+        stacked = jnp.concatenate(
+            [weight[s * group : (s + 1) * group] for weight in weights], 0
+        ).astype(jnp.bfloat16)
+        routed = lax.dot_general(
+            table, stacked, (((1,), (1,)), ((), ())), preferred_element_type=jnp.float32
+        )
+        at = pl.multiple_of((s * heads + head) * share, share)
+        sent_ref[:, pl.ds(at, share), :] = routed.reshape(holders, share, in_block * group)
+
+    @pl.when(head == heads - 1)
+    def _():
+        for holder in range(holders):
+            wire_ref[holder] = sent_ref[holder].T.astype(jnp.bfloat16)
+
+
+def gather_kernel(share, weight_ref, tile_ref, part_ref):
+    rows, lanes = part_ref.shape[1], weight_ref.shape[2]
+    weight = weight_ref[0].astype(jnp.float32)
+    in_block = tile_ref.shape[1] // HEAD_SIZE
+    group = weight.shape[0] // in_block
+    same = (
+        lax.broadcasted_iota(jnp.int32, (rows, lanes), 0) // group
+        == lax.broadcasted_iota(jnp.int32, (rows, lanes), 1) // share
+    )
+    total = jnp.zeros((rows, HEAD_SIZE), jnp.float32)
+    for j in range(in_block):
+        piece = weight[j * group : (j + 1) * group]
+        spread = jnp.where(same, jnp.concatenate([piece] * (rows // group), 0), 0.0)
+        total = total + jnp.dot(
+            spread.astype(jnp.bfloat16),
+            tile_ref[:, j * HEAD_SIZE : (j + 1) * HEAD_SIZE],
+            preferred_element_type=jnp.float32,
+        )
+    part_ref[0] = total.astype(jnp.bfloat16)
+
+
+def routed_device(
+    queries, new_keys, incoming_values, key_left, right_key_factor, value_tile_store, slot_map,
+    chosen, lengths,
+):
+    holders = lax.axis_size("store")
+    steps, _, heads, picks = chosen.shape
+    blocks = slot_map.shape[2]
+    share = max(1, blocks // holders // 4)
+    pool_here = value_tile_store.shape[0]
+    group = queries.shape[2] // HEAD_SIZE // heads
+    rank = key_left.shape[2]
+    slots = steps * heads * share
+    total = holders * share
+    keeper = slot_map[0] // pool_here
+    inside = slot_map[0] % pool_here
+    place, request = pl.pallas_call(
+        functools.partial(plan_kernel, share),
+        out_shape=(
+            jax.ShapeDtypeStruct((steps * heads, blocks), jnp.int32),
+            jax.ShapeDtypeStruct((steps * heads, total), jnp.int32),
+        ),
+        name="plan",
+    )(chosen[:, 0].reshape(steps * heads, picks), keeper, inside)
+    request = request.reshape(steps * heads, holders, share).transpose(1, 0, 2)
+    asked = lax.all_to_all(
+        request.reshape(holders, slots), "store", split_axis=0, concat_axis=0, tiled=True
+    )
+
+    length = lengths[0]
+    query = apply_rotary(
+        queries[:, 0].reshape(steps, heads * group, HEAD_SIZE).astype(jnp.float32),
+        (length + jnp.arange(steps, dtype=jnp.int32))[:, None],
+    ).astype(jnp.bfloat16)
+    query = query.reshape(steps, heads, group, HEAD_SIZE).transpose(1, 0, 2, 3)
+    query = query.reshape(heads, steps * group, HEAD_SIZE)
+    fresh_key = apply_rotary(
+        new_keys[:, 0].reshape(steps, heads, HEAD_SIZE).astype(jnp.float32),
+        (length + jnp.arange(steps, dtype=jnp.int32))[:, None],
+    ).astype(jnp.bfloat16)
+    extra = ((0, 0), (0, 8 - steps), (0, 0))
+    fresh_key = jnp.pad(fresh_key.transpose(1, 0, 2), extra)
+    fresh_value = jnp.pad(
+        incoming_values[:, 0].reshape(steps, heads, HEAD_SIZE).transpose(1, 0, 2), extra
+    )
+    left = key_left[0].reshape(blocks, BLOCK_TOKENS, rank).transpose(1, 0, 2)
+
+    half = HEAD_SIZE // 2
+    inverse = ROPE_BASE ** (-(jnp.arange(half, dtype=jnp.float32) * 2.0 / HEAD_SIZE))
+    inverse = jnp.concatenate([inverse, inverse])
+    span = 8 * BLOCK_TOKENS
+    coarse = (jnp.arange(blocks // 8, dtype=jnp.int32) * span).astype(jnp.float32)[:, None] * inverse
+    fine = (
+        jnp.arange(BLOCK_TOKENS, dtype=jnp.int32)[:, None]
+        + jnp.arange(8, dtype=jnp.int32)[None, :] * BLOCK_TOKENS
+    ).astype(jnp.float32)[..., None] * inverse
+    whole = lambda *shape: pl.BlockSpec(shape, lambda h: (0,) * len(shape))
+    per_head = lambda *shape: pl.BlockSpec((1,) + shape, lambda h: (h, 0, 0))
+    wire, fresh = pl.pallas_call(
+        functools.partial(weigh_kernel, share),
+        grid=(heads,),
+        in_specs=[
+            pl.BlockSpec(memory_space=pltpu.SMEM),
+            per_head(steps * group, HEAD_SIZE),
+            per_head(8, HEAD_SIZE),
+            per_head(8, HEAD_SIZE),
+            whole(BLOCK_TOKENS, blocks, rank),
+            pl.BlockSpec((rank, HEAD_SIZE), lambda h: (0, h)),
+            per_head(steps, blocks),
+            whole(blocks // 8, HEAD_SIZE),
+            whole(blocks // 8, HEAD_SIZE),
+            whole(BLOCK_TOKENS, 8, HEAD_SIZE),
+            whole(BLOCK_TOKENS, 8, HEAD_SIZE),
+        ],
+        out_specs=(
+            whole(holders, BLOCK_TOKENS * group, slots),
+            per_head(steps * group, HEAD_SIZE),
+        ),
+        out_shape=(
+            jax.ShapeDtypeStruct((holders, BLOCK_TOKENS * group, slots), jnp.bfloat16),
+            jax.ShapeDtypeStruct((heads, steps * group, HEAD_SIZE), jnp.float32),
+        ),
+        scratch_shapes=[
+            pltpu.VMEM((BLOCK_TOKENS, blocks, HEAD_SIZE), jnp.float32),
+            pltpu.VMEM((BLOCK_TOKENS, blocks, HEAD_SIZE), jnp.float32),
+            pltpu.VMEM((holders, slots, BLOCK_TOKENS * group), jnp.float32),
+        ],
+        cost_estimate=pl.CostEstimate(
+            flops=4 * heads * blocks * BLOCK_TOKENS * rank * HEAD_SIZE,
+            bytes_accessed=8 << 20,
+            transcendentals=0,
+        ),
+        name="weigh",
+    )(
+        lengths, query, fresh_key, fresh_value, left, right_key_factor[0],
+        place.reshape(steps, heads, blocks).transpose(1, 0, 2),
+        jnp.cos(coarse), jnp.sin(coarse), jnp.cos(fine), jnp.sin(fine),
+    )
+    got = lax.all_to_all(wire, "store", split_axis=0, concat_axis=0, tiled=True)
+    tiles = jnp.take(value_tile_store, asked.reshape(-1), axis=0)
+    rows = steps * heads * group
+    part = pl.pallas_call(
+        functools.partial(gather_kernel, share),
+        grid=(holders,),
+        in_specs=[
+            per_head(BLOCK_TOKENS * group, slots),
+            pl.BlockSpec((slots, BLOCK_TOKENS * HEAD_SIZE), lambda h: (h, 0)),
+        ],
+        out_specs=per_head(rows, HEAD_SIZE),
+        out_shape=jax.ShapeDtypeStruct((holders, rows, HEAD_SIZE), jnp.bfloat16),
+        name="partial",
+    )(got, tiles)
+    back = lax.all_to_all(part, "store", split_axis=0, concat_axis=0, tiled=True)
+    summed = jnp.sum(back.astype(jnp.float32), 0).reshape(steps, heads, group, HEAD_SIZE)
+    fresh = fresh.reshape(heads, steps, group, HEAD_SIZE).transpose(1, 0, 2, 3)
+    return (summed + fresh).astype(jnp.bfloat16).reshape(steps, 1, -1)
+
+
 def solution(mesh):
     in_specs = (
         P(None, ("groups", "store"), None),
@@ -190,6 +463,10 @@
         P(("groups", "store")),
     )
     out_specs = P(None, ("groups", "store"), None)
+    def body(*args):
+        share = max(1, args[6].shape[2] // mesh.shape["store"] // 4)
+        return (routed_device if share == 8 else per_device)(*args)
+
     return jax.shard_map(
-        per_device, mesh=mesh, in_specs=in_specs, out_specs=out_specs, check_vma=False
-    )
+        body, mesh=mesh, in_specs=in_specs, out_specs=out_specs, check_vma=False
+    )

time: 158 us -> 115 us (0.73)
  the two profiles are of different devices: /device:TPU:11 before, /device:TPU:0 now
where the time goes in v1:
time: 115 us; the launch traced here: 114 us
  Pallas kernels  43.5 us (38%)
  local copies, waits for them, and re-layouts  26.5 us (23%)
  blocking collectives  20.3 us (18%)
  starting transfers between devices  13.4 us (12%)
  other arithmetic  9.53 us (8%)
    pallas_call x1, Pallas kernels, routed_device(): pl.pallas_call(functools.partial(weigh_kernel, share), grid=(heads,), in_...  29.9 us
    all_to_all x1, blocking collectives, routed_device(): lax.all_to_all(part, 'store', split_axis=0, concat_axis=0, tiled=True)  20.3 us
    gather x1, local copies, waits for them, and re-layouts, routed_device(): tiles = jnp.take(value_tile_store, asked.reshape(-1), axis=0)  15.4 us
    pallas_call x1, Pallas kernels, routed_device(): pl.pallas_call(functools.partial(gather_kernel, share), grid=(holders,),...  11 us
    all_to_all x1, starting transfers between devices, routed_device(): lax.all_to_all(request.reshape(holders, slots), 'store', split_axis=0, co...  7.39 us
    all_to_all x1, starting transfers between devices, routed_device(): got = lax.all_to_all(wire, 'store', split_axis=0, concat_axis=0, tiled=True)  6.03 us
    select_n x2, other arithmetic, routed_device(): tiles = jnp.take(value_tile_store, asked.reshape(-1), axis=0)  3.83 us
    unnamed x6, local copies, waits for them, and re-layouts  3.81 us
  transfers between devices with their start and end apart: 2, of which 0 were waited for; matrix products, arithmetic and copies ran while one was open for 28% of the time, Pallas kernels for 26%

profile of v1, /device:TPU:0, one launch (start us, length us, event | category | flops | bytes accessed | tf_op | source)
XLA Modules:
  0.0 113.9 jit_solution(12945135514800654616)
XLA Ops:
  0.0 1.3 %add_select_fusion = (s32[8,512]{1,0:T(8,128)}, s32[8,512]{1,0:T(8,128)}) fusion(s32[1,8,512]{2,1,0:T(8,128)} %param.15), kind=kLoop, calls=%fused_computation.20 | loop fusion | flops 77824 | bytes 49152 | tf_op jit(solution)/shard_map/jit(remainder)/select_n | solution.py:350
  1.3 2.6 %plan.1 = (s32[16,512]{1,0:T(8,128)}, s32[16,128]{1,0:T(8,128)}) custom-call(s32[16,64]{1,0:T(8,128)} %bitcast.90, s32[8,512]{1,0:T(8,128)} %get-tuple-element.16.keeper_ref, s32[8,512]{1,0:T(8,128)} %get-tuple-element.15.inside_ref), custom_call_target="tpu_custom_call" | custom-call | tf_op jit(solution)/shard_map/plan/pallas_call | solution.py:351
  3.9 0.8 copy.31
  4.7 0.1 copy.32
  4.8 0.7 copy.33
  5.5 7.4 %all-to-all-start.1 = ((s32[16,1,128]{2,1,0:T(1,128)}), s32[16,1,128]{2,1,0:T(1,128)S(1)}, u32[]{:S(2)}, u32[]{:S(2)}) async-start(s32[16,1,128]{2,1,0:T(1,128)} %copy.33), calls=%async_computation.1 | async-start | bytes 16384 | tf_op jit(solution)/shard_map/all_to_all | solution.py:360
  13.6 0.1 pad_maximum_fusion
  13.6 0.1 multiply_cosine_fusion.2
  13.8 0.7 bitcast_convert_fusion
  14.4 0.1 subtract_convert_fusion.1
  14.5 0.1 maximum_bitcast_fusion.1
  14.6 0.6 pad.7.fresh_key_ref
  15.2 1.3 %pad.8.fresh_value_ref = bf16[8,8,128]{2,1,0:T(8,128)(2,1)} pad(bf16[8,2,128]{2,1,0:T(2,128)(2,1)} %bitcast.91, bf16[]{:T(256)} %constant.47.clone.1), padding=0_0x0_6x0_0 | pad | bytes 20482 | tf_op jit(solution)/shard_map/jit(_pad)/pad | solution.py:377
  16.5 1.4 %copy.43 = s32[2,8,512]{2,0,1:T(2,128)} copy(s32[2,8,512]{2,1,0:T(8,128)} %bitcast.87) | data formatting | bytes 65536 | tf_op jit(solution)/shard_map/reshape | solution.py:430
  17.9 0.8 multiply_sine_fusion
  18.7 0.8 multiply_sine_fusion.1
  19.5 0.8 convert_bitcast_fusion
  20.3 0.1 fusion.1
  20.4 3.1 %copy.28 = bf16[1,4096,160]{2,1,0:T(8,128)(2,1)S(1)} copy(bf16[1,4096,160]{1,2,0:T(8,128)(2,1)} %param.12) | data formatting | bytes 2621440 | tf_op args[3]
  23.5 1.7 %copy.41 = bf16[512,8,160]{2,0,1:T(8,128)(2,1)} copy(bf16[512,8,160]{2,1,0:T(8,128)(2,1)S(1)} %bitcast.80) | data formatting | bytes 2621440 | tf_op jit(solution)/shard_map/reshape;squeeze | solution.py:380
  25.3 0.7 copy_bitcast_fusion.3.query_ref
  26.0 29.9 %weigh.1 = (bf16[16,64,128]{2,1,0:T(8,128)(2,1)}, f32[8,16,128]{2,1,0:T(8,128)}) custom-call(s32[1]{0:T(128)} %copy.44.length_ref, bf16[8,16,128]{2,1,0:T(8,128)(2,1)} %copy_bitcast_fusion.3.query_ref, bf16[8,8,128]{2,1,0:T(8,128)(2,1)} %pad.7.fresh_key_ref, bf16[8,8,128]{2,1,0:T(8,128)(2,1)} %pad.8.fresh_value_ref, bf16[8,512,160]{2,1,0:T(8,128)(2,1)} %bitcast.81, ...), custom_call_target="tpu_custom_call" | custom-call | flops 2684354560 | bytes 8388608 | tf_op jit(solution)/shard_map/weigh/pallas_call | solution.py:393
  55.9 0.0 all-to-all-done.1
  55.9 6.0 %all-to-all-start = ((bf16[16,64,128]{2,1,0:T(8,128)(2,1)}), bf16[16,64,128]{2,1,0:T(8,128)(2,1)S(1)}, u32[]{:S(2)}, u32[]{:S(2)}) async-start(bf16[16,64,128]{2,1,0:T(8,128)(2,1)} %get-tuple-element.10), calls=%async_computation | async-start | bytes 524288 | tf_op jit(solution)/shard_map/all_to_all | solution.py:433
  62.0 15.4 %gather_fusion = bf16[2048,1024]{1,0:T(8,128)(2,1)} fusion(bf16[4096,1024]{1,0:T(8,128)(2,1)} %param.14, s32[2048]{0:T(1024)S(1)} %broadcast_clamp_fusion), kind=kCustom, calls=%fused_computation | custom fusion | bytes 8396800 | tf_op jit(solution)/shard_map/jit(_take)/gather | solution.py:434
  77.4 3.8 %broadcast_select_fusion.tile_ref = bf16[2048,1024]{1,0:T(8,128)(2,1)} fusion(bf16[2048,1024]{1,0:T(8,128)(2,1)} %gather_fusion, pred[2048]{0:T(1024)(128)(4,1)S(1)} %compare_and_fusion), kind=kLoop, calls=%fused_computation.1 | loop fusion | flops 2097152 | bytes 8390656 | tf_op jit(solution)/shard_map/jit(_take)/select_n | solution.py:434
  81.2 0.0 copy-start.1
  81.2 0.0 all-to-all-done.weight_ref
  81.2 0.0 copy-start
  81.3 0.7 copy-done
  82.0 11.0 %partial.1 = bf16[16,128,128]{2,1,0:T(8,128)(2,1)} custom-call(bf16[16,64,128]{2,1,0:T(8,128)(2,1)} %copy-done, bf16[2048,1024]{1,0:T(8,128)(2,1)} %broadcast_select_fusion.tile_ref), custom_call_target="tpu_custom_call" | custom-call | tf_op jit(solution)/shard_map/partial/pallas_call | solution.py:436
  92.9 20.3 %all_to_all.19 = bf16[16,128,128]{2,1,0:T(8,128)(2,1)S(1)} all-to-all(bf16[16,128,128]{2,1,0:T(8,128)(2,1)} %partial.1), channel_id=1, replica_groups=mesh['groups'=2,'store'=16] {'store'}, dimensions={0} | all-to-all | bytes 1048576 | tf_op jit(solution)/shard_map/all_to_all | solution.py:447
  113.2 0.1 convert_reduce_fusion
  113.3 0.0 copy-done.1
  113.3 0.6 reshape.182
  (10 shorter events, 0.1 us)
Async XLA Ops:
  5.5 50.5 %all-to-all-start.1 = ((s32[16,1,128]{2,1,0:T(1,128)}), s32[16,1,128]{2,1,0:T(1,128)S(1)}, u32[]{:S(2)}, u32[]{:S(2)}) async-start(s32[16,1,128]{2,1,0:T(1,128)} %copy.33), calls=%async_computation.1 | async-start | bytes 16384 | tf_op jit(solution)/shard_map/all_to_all | solution.py:360
  55.9 25.3 %all-to-all-start = ((bf16[16,64,128]{2,1,0:T(8,128)(2,1)}), bf16[16,64,128]{2,1,0:T(8,128)(2,1)S(1)}, u32[]{:S(2)}, u32[]{:S(2)}) async-start(bf16[16,64,128]{2,1,0:T(8,128)(2,1)} %get-tuple-element.10), calls=%async_computation | async-start | bytes 524288 | tf_op jit(solution)/shard_map/all_to_all | solution.py:433
  81.2 32.0 %copy-start.1 = (f32[8,16,128]{2,1,0:T(8,128)S(1)}, f32[8,16,128]{2,1,0:T(8,128)}, u32[]{:S(2)}) copy-start(f32[8,16,128]{2,1,0:T(8,128)} %get-tuple-element.12) | copy-start | bytes 196612
  81.2 0.7 copy-start

commit v2 on v1

--- a/solution.py
+++ b/solution.py
@@ -312,25 +312,105 @@
             wire_ref[holder] = sent_ref[holder].T.astype(jnp.bfloat16)
 
 
-def gather_kernel(share, weight_ref, tile_ref, part_ref):
-    rows, lanes = part_ref.shape[1], weight_ref.shape[2]
-    weight = weight_ref[0].astype(jnp.float32)
-    in_block = tile_ref.shape[1] // HEAD_SIZE
-    group = weight.shape[0] // in_block
+def meet_kernel(
+    share, wire_ref, fresh_ref, tiles_ref, out_ref,
+    got_ref, part_ref, back_ref, block_ref,
+    tile_sem, weight_send, weight_recv, part_send, part_recv,
+):
+    holders, lines, lanes = wire_ref.shape
+    rows = out_ref.shape[0]
+    in_block = block_ref.shape[2] // HEAD_SIZE
+    group = lines // in_block
+    me = lax.axis_index("store")
+
+    def tile_copy(k):
+        source = lax.rem(me - k + holders, holders)
+        return pltpu.make_async_copy(
+            tiles_ref.at[pl.ds(pl.multiple_of(source * lanes, lanes), lanes)],
+            block_ref.at[k],
+            tile_sem.at[k],
+        )
+
+    def weight_copy(k):
+        peer = lax.rem(me + k, holders)
+        return pltpu.make_async_remote_copy(
+            src_ref=wire_ref.at[peer],
+            dst_ref=got_ref.at[k],
+            send_sem=weight_send.at[k],
+            recv_sem=weight_recv.at[k],
+            device_id={"store": peer},
+            device_id_type=pl.DeviceIdType.MESH,
+        )
+
+    def part_copy(k):
+        peer = lax.rem(me - k + holders, holders)
+        return pltpu.make_async_remote_copy(
+            src_ref=part_ref.at[k],
+            dst_ref=back_ref.at[k],
+            send_sem=part_send.at[k],
+            recv_sem=part_recv.at[k],
+            device_id={"store": peer},
+            device_id_type=pl.DeviceIdType.MESH,
+        )
+
+    barrier = pltpu.get_barrier_semaphore()
+
+    def greet(k, _):
+        pl.semaphore_signal(
+            barrier, inc=1, device_id={"store": lax.rem(me + k, holders)},
+            device_id_type=pl.DeviceIdType.MESH,
+        )
+        return 0
+
+    lax.fori_loop(1, holders, greet, 0)
+    for k in range(holders):
+        tile_copy(k).start()
+    pl.semaphore_wait(barrier, holders - 1)
+    for k in range(1, holders):
+        weight_copy(k).start()
+
     same = (
         lax.broadcasted_iota(jnp.int32, (rows, lanes), 0) // group
         == lax.broadcasted_iota(jnp.int32, (rows, lanes), 1) // share
     )
-    total = jnp.zeros((rows, HEAD_SIZE), jnp.float32)
-    for j in range(in_block):
-        piece = weight[j * group : (j + 1) * group]
-        spread = jnp.where(same, jnp.concatenate([piece] * (rows // group), 0), 0.0)
-        total = total + jnp.dot(
-            spread.astype(jnp.bfloat16),
-            tile_ref[:, j * HEAD_SIZE : (j + 1) * HEAD_SIZE],
-            preferred_element_type=jnp.float32,
-        )
-    part_ref[0] = total.astype(jnp.bfloat16)
+
+    def partial(weight, k):
+        total = jnp.zeros((rows, HEAD_SIZE), jnp.float32)
+        weight = weight.astype(jnp.float32)
+        for j in range(in_block):
+            piece = weight[j * group : (j + 1) * group]
+            spread = jnp.where(same, jnp.concatenate([piece] * (rows // group), 0), 0.0)
+            total = total + jnp.dot(
+                spread.astype(jnp.bfloat16),
+                block_ref[k, :, j * HEAD_SIZE : (j + 1) * HEAD_SIZE],
+                preferred_element_type=jnp.float32,
+            )
+        return total
+
+    tile_copy(0).wait()
+    own = partial(wire_ref[me], 0) + fresh_ref[...]
+
+    def answer(k, _):
+        tile_copy(k).wait()
+        weight_copy(k).wait_recv()
+        part_ref[k] = partial(got_ref[k], k).astype(jnp.bfloat16)
+        part_copy(k).start()
+        return 0
+
+    lax.fori_loop(1, holders, answer, 0)
+
+    def collect(k, total):
+        part_copy(k).wait_recv()
+        return total + back_ref[k].astype(jnp.float32)
+
+    out_ref[...] = lax.fori_loop(1, holders, collect, own).astype(jnp.bfloat16)
+
+    def finish(k, _):
+        weight_copy(k).wait_send()
+        part_copy(k).wait_send()
+        return 0
+
+    lax.fori_loop(1, holders, finish, 0)
 
 
 def routed_device(
@@ -430,24 +510,27 @@
         place.reshape(steps, heads, blocks).transpose(1, 0, 2),
         jnp.cos(coarse), jnp.sin(coarse), jnp.cos(fine), jnp.sin(fine),
     )
-    got = lax.all_to_all(wire, "store", split_axis=0, concat_axis=0, tiled=True)
-    tiles = jnp.take(value_tile_store, asked.reshape(-1), axis=0)
+    tiles = value_tile_store.at[asked.reshape(-1)].get(mode="promise_in_bounds")
     rows = steps * heads * group
-    part = pl.pallas_call(
-        functools.partial(gather_kernel, share),
-        grid=(holders,),
-        in_specs=[
-            per_head(BLOCK_TOKENS * group, slots),
-            pl.BlockSpec((slots, BLOCK_TOKENS * HEAD_SIZE), lambda h: (h, 0)),
-        ],
-        out_specs=per_head(rows, HEAD_SIZE),
-        out_shape=jax.ShapeDtypeStruct((holders, rows, HEAD_SIZE), jnp.bfloat16),
-        name="partial",
-    )(got, tiles)
-    back = lax.all_to_all(part, "store", split_axis=0, concat_axis=0, tiled=True)
-    summed = jnp.sum(back.astype(jnp.float32), 0).reshape(steps, heads, group, HEAD_SIZE)
     fresh = fresh.reshape(heads, steps, group, HEAD_SIZE).transpose(1, 0, 2, 3)
-    return (summed + fresh).astype(jnp.bfloat16).reshape(steps, 1, -1)
+    lines = BLOCK_TOKENS * group
+    in_vmem = pl.BlockSpec(memory_space=pltpu.VMEM)
+    attended = pl.pallas_call(
+        functools.partial(meet_kernel, share),
+        in_specs=[in_vmem, in_vmem, pl.BlockSpec(memory_space=pl.ANY)],
+        out_specs=in_vmem,
+        out_shape=jax.ShapeDtypeStruct((rows, HEAD_SIZE), jnp.bfloat16),
+        scratch_shapes=[
+            pltpu.VMEM((holders, lines, slots), jnp.bfloat16),
+            pltpu.VMEM((holders, rows, HEAD_SIZE), jnp.bfloat16),
+            pltpu.VMEM((holders, rows, HEAD_SIZE), jnp.bfloat16),
+            pltpu.VMEM((holders, slots, BLOCK_TOKENS * HEAD_SIZE), jnp.bfloat16),
+        ]
+        + [pltpu.SemaphoreType.DMA((holders,))] * 5,
+        compiler_params=pltpu.CompilerParams(collective_id=0, has_side_effects=True),
+        name="meet",
+    )(wire, fresh.reshape(rows, HEAD_SIZE), tiles)
+    return attended.reshape(steps, 1, -1)
 
 
 def solution(mesh):

time: 115 us -> 104 us (0.904)
  blocking collectives: 20.3 us -> 0 us
  Pallas kernels: 43.5 us -> 61.2 us
  starting transfers between devices: 13.4 us -> 7.38 us
  other arithmetic: 9.53 us -> 5.63 us
  local copies, waits for them, and re-layouts: 26.5 us -> 27.9 us
    all_to_all x1 -> x0, blocking collectives: 20.3 us -> none  [routed_device(): lax.all_to_all(part, 'store', split_axis=0, concat_axis=0, tiled=True)]
    pallas_call x1, Pallas kernels: 11 us -> 28.7 us  [routed_device(): pl.pallas_call(functools.partial(meet_kernel, share), in_specs=[in_vmem,...]
    all_to_all x1 -> x0, starting transfers between devices: 6.03 us -> none  [routed_device(): got = lax.all_to_all(wire, 'store', split_axis=0, concat_axis=0, tiled=True)]
    select_n x2 -> x1, other arithmetic: 3.83 us -> 0.01 us  [routed_device(): tiles = value_tile_store.at[asked.reshape(-1)].get(mode='promise_in_bounds')]
    reshape x1 -> x2, local copies, waits for them, and re-layouts: 0.63 us -> 2.85 us  [the longest x1 1.46 us: routed_device(): fresh = fresh.reshape(heads, steps, group, HEAD_SIZE).transpose(1, 0, 2, 3)]
    unnamed x6 -> x2, local copies, waits for them, and re-layouts: 3.81 us -> 3.1 us
  transfers between devices with their start and end apart: 2 -> 1, of which waited for: 0 -> 0; matrix products, arithmetic and copies ran while one was open for 28% -> 13% of each run, Pallas kernels for 26% -> 29%
where the time goes in v2:
time: 104 us; the launch traced here: 103 us
  Pallas kernels  61.2 us (59%)
  local copies, waits for them, and re-layouts  27.9 us (27%)
  starting transfers between devices  7.38 us (7%)
  other arithmetic  5.63 us (5%)
    pallas_call x1, Pallas kernels, routed_device(): pl.pallas_call(functools.partial(weigh_kernel, share), grid=(heads,), in_...  29.9 us
    pallas_call x1, Pallas kernels, routed_device(): pl.pallas_call(functools.partial(meet_kernel, share), in_specs=[in_vmem,...  28.7 us
    gather x1, local copies, waits for them, and re-layouts, routed_device(): tiles = value_tile_store.at[asked.reshape(-1)].get(mode='promise_in_bounds')  15.4 us
    all_to_all x1, starting transfers between devices, routed_device(): lax.all_to_all(request.reshape(holders, slots), 'store', split_axis=0, co...  7.38 us
    unnamed x2, local copies, waits for them, and re-layouts  3.1 us
    pallas_call x1, Pallas kernels, routed_device(): pl.pallas_call(functools.partial(plan_kernel, share), out_shape=(jax.Shap...  2.57 us
  transfers between devices with their start and end apart: 1, of which 0 were waited for; matrix products, arithmetic and copies ran while one was open for 13% of the time, Pallas kernels for 29%

profile of v2, /device:TPU:0, one launch (start us, length us, event | category | flops | bytes accessed | tf_op | source)
XLA Modules:
  0.0 102.8 jit_solution(15202277653520482910)
XLA Ops:
  0.0 1.3 %add_select_fusion = (s32[8,512]{1,0:T(8,128)}, s32[8,512]{1,0:T(8,128)}) fusion(s32[1,8,512]{2,1,0:T(8,128)} %param.15), kind=kLoop, calls=%fused_computation.16 | loop fusion | flops 77824 | bytes 49152 | tf_op jit(solution)/shard_map/jit(remainder)/select_n | solution.py:430
  1.3 2.6 %plan.1 = (s32[16,512]{1,0:T(8,128)}, s32[16,128]{1,0:T(8,128)}) custom-call(s32[16,64]{1,0:T(8,128)} %bitcast.83, s32[8,512]{1,0:T(8,128)} %get-tuple-element.16.keeper_ref, s32[8,512]{1,0:T(8,128)} %get-tuple-element.15.inside_ref), custom_call_target="tpu_custom_call" | custom-call | tf_op jit(solution)/shard_map/plan/pallas_call | solution.py:431
  3.9 0.8 copy.31
  4.7 0.1 copy.32
  4.8 0.7 copy.33
  5.5 7.4 %all-to-all-start = ((s32[16,1,128]{2,1,0:T(1,128)}), s32[16,1,128]{2,1,0:T(1,128)S(1)}, u32[]{:S(2)}, u32[]{:S(2)}) async-start(s32[16,1,128]{2,1,0:T(1,128)} %copy.33), calls=%async_computation | async-start | bytes 16384 | tf_op jit(solution)/shard_map/all_to_all | solution.py:440
  13.5 0.1 pad_maximum_fusion
  13.6 0.1 multiply_cosine_fusion.2
  13.7 0.7 bitcast_convert_fusion
  14.4 0.1 subtract_convert_fusion.1
  14.5 0.1 maximum_bitcast_fusion.1
  14.6 0.6 pad.7.fresh_key_ref
  15.2 1.3 %pad.8.fresh_value_ref = bf16[8,8,128]{2,1,0:T(8,128)(2,1)} pad(bf16[8,2,128]{2,1,0:T(2,128)(2,1)} %bitcast.84, bf16[]{:T(256)} %constant.36.clone.1), padding=0_0x0_6x0_0 | pad | bytes 20482 | tf_op jit(solution)/shard_map/jit(_pad)/pad | solution.py:457
  16.5 1.4 %copy.41 = s32[2,8,512]{2,0,1:T(2,128)} copy(s32[2,8,512]{2,1,0:T(8,128)} %bitcast.80) | data formatting | bytes 65536 | tf_op jit(solution)/shard_map/reshape | solution.py:510
  17.9 0.8 multiply_sine_fusion
  18.7 0.8 multiply_sine_fusion.1
  19.5 0.8 convert_bitcast_fusion
  20.3 0.1 fusion
  20.4 3.1 %copy.27 = bf16[1,4096,160]{2,1,0:T(8,128)(2,1)S(1)} copy(bf16[1,4096,160]{1,2,0:T(8,128)(2,1)} %param.12) | data formatting | bytes 2621440 | tf_op args[3]
  23.5 1.8 %copy.39 = bf16[512,8,160]{2,0,1:T(8,128)(2,1)} copy(bf16[512,8,160]{2,1,0:T(8,128)(2,1)S(1)} %bitcast.73) | data formatting | bytes 2621440 | tf_op jit(solution)/shard_map/reshape;squeeze | solution.py:460
  25.3 0.7 copy_bitcast_fusion.3.query_ref
  26.0 29.9 %weigh.1 = (bf16[16,64,128]{2,1,0:T(8,128)(2,1)}, f32[8,16,128]{2,1,0:T(8,128)}) custom-call(s32[1]{0:T(128)} %copy.42.length_ref, bf16[8,16,128]{2,1,0:T(8,128)(2,1)} %copy_bitcast_fusion.3.query_ref, bf16[8,8,128]{2,1,0:T(8,128)(2,1)} %pad.7.fresh_key_ref, bf16[8,8,128]{2,1,0:T(8,128)(2,1)} %pad.8.fresh_value_ref, bf16[8,512,160]{2,1,0:T(8,128)(2,1)} %bitcast.74, ...), custom_call_target="tpu_custom_call" | custom-call | flops 2684354560 | bytes 8388608 | tf_op jit(solution)/shard_map/weigh/pallas_call | solution.py:473
  55.9 1.5 %copy.30 = f32[8,2,8,128]{3,2,0,1:T(8,128)} copy(f32[8,2,8,128]{3,2,1,0:T(8,128)} %bitcast.79) | data formatting | bytes 131072 | tf_op jit(solution)/shard_map/reshape | solution.py:515
  57.4 0.0 all-to-all-done
  57.4 15.4 %gather_fusion = bf16[2048,1024]{1,0:T(8,128)(2,1)} fusion(bf16[4096,1024]{1,0:T(8,128)(2,1)} %param.14, s32[2048]{0:T(1024)S(1)} %broadcast_clamp_fusion), kind=kCustom, calls=%fused_computation | custom fusion | bytes 8396800 | tf_op jit(solution)/shard_map/gather | solution.py:513
  72.8 28.7 %meet.1 = bf16[128,128]{1,0:T(8,128)(2,1)} custom-call(bf16[16,64,128]{2,1,0:T(8,128)(2,1)} %get-tuple-element.10.wire_ref, f32[128,128]{1,0:T(8,128)} %bitcast.76, bf16[2048,1024]{1,0:T(8,128)(2,1)} %gather_fusion), custom_call_target="tpu_custom_call" | custom-call | tf_op jit(solution)/shard_map/meet/pallas_call | solution.py:518
  101.5 1.4 %reshape.172 = bf16[2,1,8192]{2,0,1:T(2,128)(2,1)} reshape(bf16[128,128]{1,0:T(8,128)(2,1)} %meet.1) | data formatting | bytes 65536 | tf_op jit(solution)/shard_map/reshape | solution.py:533
  (8 shorter events, 0.0 us)
Async XLA Ops:
  5.5 51.9 %all-to-all-start = ((s32[16,1,128]{2,1,0:T(1,128)}), s32[16,1,128]{2,1,0:T(1,128)S(1)}, u32[]{:S(2)}, u32[]{:S(2)}) async-start(s32[16,1,128]{2,1,0:T(1,128)} %copy.33), calls=%async_computation | async-start | bytes 16384 | tf_op jit(solution)/shard_map/all_to_all | solution.py:440

commit v3 on v2

--- a/solution.py
+++ b/solution.py
@@ -2,6 +2,7 @@
 
 import jax
 import jax.numpy as jnp
+import numpy as np
 from jax import lax
 from jax.experimental import pallas as pl
 from jax.experimental.pallas import tpu as pltpu
@@ -227,87 +228,93 @@
 def weigh_kernel(
     share, length_ref, query_ref, fresh_key_ref, fresh_value_ref, left_ref, right_ref, place_ref,
     coarse_cos_ref, coarse_sin_ref, fine_cos_ref, fine_sin_ref,
-    wire_ref, fresh_ref, cos_ref, sin_ref, sent_ref,
+    wire_ref, fresh_ref, raw_ref, score_ref, sent_ref,
 ):
-    head = pl.program_id(0)
-    heads = pl.num_programs(0)
-    in_block, blocks, _ = left_ref.shape
+    j = pl.program_id(0)
+    in_block = pl.num_programs(0)
+    heads, both, _ = query_ref.shape
+    blocks = left_ref.shape[1]
     steps = place_ref.shape[1]
-    both = query_ref.shape[1]
     group = both // steps
     holders = wire_ref.shape[0]
-    length = length_ref[0]
-
-    @pl.when(head == 0)
+    half = HEAD_SIZE // 2
+    scale = HEAD_SIZE ** (-0.5)
+
+    raw_ref[...] = lax.dot_general(
+        right_ref[...], left_ref[0], (((1,), (1,)), ((), ())), preferred_element_type=jnp.float32
+    )
+    fine_cos, fine_sin = fine_cos_ref[0], fine_sin_ref[0]
+    cosine = coarse_cos_ref[...] * fine_cos - coarse_sin_ref[...] * fine_sin
+    sine = coarse_sin_ref[...] * fine_cos + coarse_cos_ref[...] * fine_sin
+    for head in range(heads):
+        first = raw_ref[head * HEAD_SIZE : head * HEAD_SIZE + half]
+        second = raw_ref[head * HEAD_SIZE + half : (head + 1) * HEAD_SIZE]
+        keys = jnp.concatenate(
+            [first * cosine - second * sine, second * cosine + first * sine], 0
+        ).astype(jnp.bfloat16)
+        score_ref[head, j] = (
+            jnp.dot(query_ref[head], keys, preferred_element_type=jnp.float32) * scale
+        )
+
+    @pl.when(j == in_block - 1)
     def _():
-        coarse_cos = coarse_cos_ref[...][:, None, :]
-        coarse_sin = coarse_sin_ref[...][:, None, :]
-        sign = jnp.where(
-            lax.broadcasted_iota(jnp.int32, (1, 1, HEAD_SIZE), 2) < HEAD_SIZE // 2, -1.0, 1.0
-        )
-        for j in range(in_block):
-            fine_cos = fine_cos_ref[j][None]
-            fine_sin = fine_sin_ref[j][None]
-            cos_ref[j] = (coarse_cos * fine_cos - coarse_sin * fine_sin).reshape(blocks, HEAD_SIZE)
-            sin_ref[j] = ((coarse_sin * fine_cos + coarse_cos * fine_sin) * sign).reshape(
-                blocks, HEAD_SIZE
+        length = length_ref[0]
+        tokens = score_ref.shape[1]
+        block_at = lax.broadcasted_iota(jnp.int32, (both, blocks), 1)
+        slot_at = lax.broadcasted_iota(jnp.int32, (holders * share, blocks), 0)
+        fresh_keep = (
+            lax.broadcasted_iota(jnp.int32, (both, 8), 1)
+            <= lax.broadcasted_iota(jnp.int32, (both, 8), 0) // group
+        )
+
+        def one_head(head, _):
+            query = query_ref[head]
+            place = place_ref[head]
+            place_rows = jnp.concatenate(
+                [jnp.broadcast_to(place[s : s + 1], (group, blocks)) for s in range(steps)], 0
             )
-
-    query = query_ref[0]
-    place = place_ref[0]
-    place_rows = jnp.concatenate(
-        [jnp.broadcast_to(place[s : s + 1], (group, blocks)) for s in range(steps)], 0
-    )
-    block_at = lax.broadcasted_iota(jnp.int32, (both, blocks), 1)
-    scale = HEAD_SIZE ** (-0.5)
-    scores = []
-    for j in range(in_block):
-        raw = jnp.dot(left_ref[j], right_ref[...], preferred_element_type=jnp.float32)
-        keys = (
-            raw * cos_ref[j] + pltpu.roll(raw, HEAD_SIZE // 2, 1) * sin_ref[j]
-        ).astype(jnp.bfloat16)
-        score = lax.dot_general(
-            query, keys, (((1,), (1,)), ((), ())), preferred_element_type=jnp.float32
-        ) * scale
-        keep = jnp.logical_and(place_rows >= 0, block_at * in_block + j < length)
-        scores.append(jnp.where(keep, score, -jnp.inf))
-    fresh = lax.dot_general(
-        query, fresh_key_ref[0], (((1,), (1,)), ((), ())), preferred_element_type=jnp.float32
-    ) * scale
-    fresh_keep = (
-        lax.broadcasted_iota(jnp.int32, fresh.shape, 1)
-        <= lax.broadcasted_iota(jnp.int32, fresh.shape, 0) // group
-    )
-    fresh = jnp.where(fresh_keep, fresh, -jnp.inf)
-    top = scores[0]
-    for j in range(1, in_block):
-        top = jnp.maximum(top, scores[j])
-    highest = jnp.maximum(
-        jnp.max(top, -1, keepdims=True), jnp.max(fresh, -1, keepdims=True)
-    )
-    powers = [jnp.exp(score - highest) for score in scores]
-    fresh_power = jnp.exp(fresh - highest)
-    total = powers[0]
-    for j in range(1, in_block):
-        total = total + powers[j]
-    denominator = jnp.sum(total, -1, keepdims=True) + jnp.sum(fresh_power, -1, keepdims=True)
-    weights = [power / denominator for power in powers]
-    fresh_weight = (fresh_power / denominator).astype(jnp.bfloat16)
-    fresh_ref[0] = jnp.dot(fresh_weight, fresh_value_ref[0], preferred_element_type=jnp.float32)
-    slot_at = lax.broadcasted_iota(jnp.int32, (holders * share, blocks), 0)
-    for s in range(steps):
-        table = jnp.where(place[s : s + 1] == slot_at, 1.0, 0.0).astype(jnp.bfloat16)
-        stacked = jnp.concatenate(
-            [weight[s * group : (s + 1) * group] for weight in weights], 0
-        ).astype(jnp.bfloat16)
-        routed = lax.dot_general(
-            table, stacked, (((1,), (1,)), ((), ())), preferred_element_type=jnp.float32
-        )
-        at = pl.multiple_of((s * heads + head) * share, share)
-        sent_ref[:, pl.ds(at, share), :] = routed.reshape(holders, share, in_block * group)
-
-    @pl.when(head == heads - 1)
-    def _():
+            inside_at = jnp.where(place_rows >= 0, block_at * tokens, length)
+            scores = [
+                jnp.where(inside_at + t < length, score_ref[head, t], -jnp.inf)
+                for t in range(tokens)
+            ]
+            fresh = lax.dot_general(
+                query, fresh_key_ref[head], (((1,), (1,)), ((), ())),
+                preferred_element_type=jnp.float32,
+            ) * scale
+            fresh = jnp.where(fresh_keep, fresh, -jnp.inf)
+            top = scores[0]
+            for t in range(1, tokens):
+                top = jnp.maximum(top, scores[t])
+            highest = jnp.maximum(
+                jnp.max(top, -1, keepdims=True), jnp.max(fresh, -1, keepdims=True)
+            )
+            powers = [jnp.exp(score - highest) for score in scores]
+            fresh_power = jnp.exp(fresh - highest)
+            total = powers[0]
+            for t in range(1, tokens):
+                total = total + powers[t]
+            denominator = jnp.sum(total, -1, keepdims=True) + jnp.sum(
+                fresh_power, -1, keepdims=True
+            )
+            weights = [power / denominator for power in powers]
+            fresh_weight = (fresh_power / denominator).astype(jnp.bfloat16)
+            fresh_ref[head] = jnp.dot(
+                fresh_weight, fresh_value_ref[head], preferred_element_type=jnp.float32
+            )
+            for s in range(steps):
+                table = jnp.where(place[s : s + 1] == slot_at, 1.0, 0.0).astype(jnp.bfloat16)
+                stacked = jnp.concatenate(
+                    [weight[s * group : (s + 1) * group] for weight in weights], 0
+                ).astype(jnp.bfloat16)
+                routed = lax.dot_general(
+                    table, stacked, (((1,), (1,)), ((), ())), preferred_element_type=jnp.float32
+                )
+                at = pl.multiple_of((s * heads + head) * share, share)
+                sent_ref[:, pl.ds(at, share), :] = routed.reshape(holders, share, tokens * group)
+            return 0
+
+        lax.fori_loop(0, heads, one_head, 0)
         for holder in range(holders):
             wire_ref[holder] = sent_ref[holder].T.astype(jnp.bfloat16)
 
@@ -460,43 +467,39 @@
     left = key_left[0].reshape(blocks, BLOCK_TOKENS, rank).transpose(1, 0, 2)
 
     half = HEAD_SIZE // 2
-    inverse = ROPE_BASE ** (-(jnp.arange(half, dtype=jnp.float32) * 2.0 / HEAD_SIZE))
-    inverse = jnp.concatenate([inverse, inverse])
-    span = 8 * BLOCK_TOKENS
-    coarse = (jnp.arange(blocks // 8, dtype=jnp.int32) * span).astype(jnp.float32)[:, None] * inverse
-    fine = (
-        jnp.arange(BLOCK_TOKENS, dtype=jnp.int32)[:, None]
-        + jnp.arange(8, dtype=jnp.int32)[None, :] * BLOCK_TOKENS
-    ).astype(jnp.float32)[..., None] * inverse
-    whole = lambda *shape: pl.BlockSpec(shape, lambda h: (0,) * len(shape))
-    per_head = lambda *shape: pl.BlockSpec((1,) + shape, lambda h: (h, 0, 0))
+    inverse = ROPE_BASE ** (-(np.arange(half, dtype=np.float32) * 2.0 / HEAD_SIZE))
+    coarse = inverse[:, None] * (np.arange(blocks) * BLOCK_TOKENS)[None, :]
+    fine = (np.arange(BLOCK_TOKENS)[:, None] * inverse[None, :])[..., None]
+    constant = lambda table: jnp.asarray(table.astype(np.float32))
+    whole = lambda *shape: pl.BlockSpec(shape, lambda j: (0,) * len(shape))
+    per_token = lambda *shape: pl.BlockSpec((1,) + shape, lambda j: (j, 0, 0))
     wire, fresh = pl.pallas_call(
         functools.partial(weigh_kernel, share),
-        grid=(heads,),
+        grid=(BLOCK_TOKENS,),
         in_specs=[
             pl.BlockSpec(memory_space=pltpu.SMEM),
-            per_head(steps * group, HEAD_SIZE),
-            per_head(8, HEAD_SIZE),
-            per_head(8, HEAD_SIZE),
-            whole(BLOCK_TOKENS, blocks, rank),
-            pl.BlockSpec((rank, HEAD_SIZE), lambda h: (0, h)),
-            per_head(steps, blocks),
-            whole(blocks // 8, HEAD_SIZE),
-            whole(blocks // 8, HEAD_SIZE),
-            whole(BLOCK_TOKENS, 8, HEAD_SIZE),
-            whole(BLOCK_TOKENS, 8, HEAD_SIZE),
+            whole(heads, steps * group, HEAD_SIZE),
+            whole(heads, 8, HEAD_SIZE),
+            whole(heads, 8, HEAD_SIZE),
+            per_token(blocks, rank),
+            whole(heads * HEAD_SIZE, rank),
+            whole(heads, steps, blocks),
+            whole(half, blocks),
+            whole(half, blocks),
+            per_token(half, 1),
+            per_token(half, 1),
         ],
         out_specs=(
             whole(holders, BLOCK_TOKENS * group, slots),
-            per_head(steps * group, HEAD_SIZE),
+            whole(heads, steps * group, HEAD_SIZE),
         ),
         out_shape=(
             jax.ShapeDtypeStruct((holders, BLOCK_TOKENS * group, slots), jnp.bfloat16),
             jax.ShapeDtypeStruct((heads, steps * group, HEAD_SIZE), jnp.float32),
         ),
         scratch_shapes=[
-            pltpu.VMEM((BLOCK_TOKENS, blocks, HEAD_SIZE), jnp.float32),
-            pltpu.VMEM((BLOCK_TOKENS, blocks, HEAD_SIZE), jnp.float32),
+            pltpu.VMEM((heads * HEAD_SIZE, blocks), jnp.float32),
+            pltpu.VMEM((heads, BLOCK_TOKENS, steps * group, blocks), jnp.float32),
             pltpu.VMEM((holders, slots, BLOCK_TOKENS * group), jnp.float32),
         ],
         cost_estimate=pl.CostEstimate(
@@ -506,9 +509,10 @@
         ),
         name="weigh",
     )(
-        lengths, query, fresh_key, fresh_value, left, right_key_factor[0],
+        lengths, query, fresh_key, fresh_value, left, right_key_factor[0].T,
         place.reshape(steps, heads, blocks).transpose(1, 0, 2),
-        jnp.cos(coarse), jnp.sin(coarse), jnp.cos(fine), jnp.sin(fine),
+        constant(np.cos(coarse)), constant(np.sin(coarse)),
+        constant(np.cos(fine)), constant(np.sin(fine)),
     )
     tiles = value_tile_store.at[asked.reshape(-1)].get(mode="promise_in_bounds")
     rows = steps * heads * group

time: 104 us -> 85.3 us (0.82)
  Pallas kernels: 61.2 us -> 44.2 us
  other arithmetic: 5.63 us -> 3.91 us
    pallas_call x1, Pallas kernels: 29.9 us -> 12.9 us  [routed_device(): pl.pallas_call(functools.partial(weigh_kernel, share), grid=(BLOCK_TOKENS...]
    sin x2 -> x0, other arithmetic: 1.63 us -> none  [the longest x1 0.82 us: routed_device(): jnp.sin(fine)]
    unnamed x2 -> x7, local copies, waits for them, and re-layouts: 3.1 us -> 4.13 us
  transfers between devices with their start and end apart: 1 -> 1, of which waited for: 0 -> 0; matrix products, arithmetic and copies ran while one was open for 13% -> 15% of each run, Pallas kernels for 29% -> 15%
where the time goes in v3:
time: 85.3 us; the launch traced here: 84.5 us
  Pallas kernels  44.2 us (52%)
  local copies, waits for them, and re-layouts  28.3 us (33%)
  starting transfers between devices  7.38 us (9%)
  other arithmetic  3.91 us (5%)
    pallas_call x1, Pallas kernels, routed_device(): pl.pallas_call(functools.partial(meet_kernel, share), in_specs=[in_vmem,...  28.7 us
    gather x1, local copies, waits for them, and re-layouts, routed_device(): tiles = value_tile_store.at[asked.reshape(-1)].get(mode='promise_in_bounds')  15.4 us
    pallas_call x1, Pallas kernels, routed_device(): pl.pallas_call(functools.partial(weigh_kernel, share), grid=(BLOCK_TOKENS...  12.9 us
    all_to_all x1, starting transfers between devices, routed_device(): lax.all_to_all(request.reshape(holders, slots), 'store', split_axis=0, co...  7.38 us
    unnamed x7, local copies, waits for them, and re-layouts  4.13 us
    pallas_call x1, Pallas kernels, routed_device(): pl.pallas_call(functools.partial(plan_kernel, share), out_shape=(jax.Shap...  2.57 us
    another operation x1, local copies, waits for them, and re-layouts, routed_device(): left = key_left[0].reshape(blocks, BLOCK_TOKENS, rank).transpose(1, 0, 2)  1.76 us
  transfers between devices with their start and end apart: 1, of which 0 were waited for; matrix products, arithmetic and copies ran while one was open for 15% of the time, Pallas kernels for 15%

profile of v3, /device:TPU:0, one launch (start us, length us, event | category | flops | bytes accessed | tf_op | source)
XLA Modules:
  0.0 84.5 jit_solution(12383360357880342205)
XLA Ops:
  0.0 1.3 %add_select_fusion = (s32[8,512]{1,0:T(8,128)}, s32[8,512]{1,0:T(8,128)}) fusion(s32[1,8,512]{2,1,0:T(8,128)} %param.19), kind=kLoop, calls=%fused_computation.12 | loop fusion | flops 77824 | bytes 49152 | tf_op jit(solution)/shard_map/jit(remainder)/select_n | solution.py:437
  1.3 2.6 %plan.1 = (s32[16,512]{1,0:T(8,128)}, s32[16,128]{1,0:T(8,128)}) custom-call(s32[16,64]{1,0:T(8,128)} %bitcast.86, s32[8,512]{1,0:T(8,128)} %get-tuple-element.16.keeper_ref, s32[8,512]{1,0:T(8,128)} %get-tuple-element.15.inside_ref), custom_call_target="tpu_custom_call" | custom-call | tf_op jit(solution)/shard_map/plan/pallas_call | solution.py:438
  3.9 0.8 copy.39
  4.7 0.0 copy-start
  4.7 0.1 copy.40
  4.8 0.7 copy.41
  5.5 7.4 %all-to-all-start = ((s32[16,1,128]{2,1,0:T(1,128)}), s32[16,1,128]{2,1,0:T(1,128)S(1)}, u32[]{:S(2)}, u32[]{:S(2)}) async-start(s32[16,1,128]{2,1,0:T(1,128)} %copy.41), calls=%async_computation | async-start | bytes 16384 | tf_op jit(solution)/shard_map/all_to_all | solution.py:447
  13.6 0.8 convert_bitcast_fusion
  14.4 0.7 bitcast_convert_fusion
  15.1 0.1 multiply_cosine_fusion
  15.2 0.1 fusion
  15.3 0.1 subtract_convert_fusion.1
  15.3 1.4 %copy.49 = s32[2,8,512]{2,0,1:T(2,128)} copy(s32[2,8,512]{2,1,0:T(8,128)} %bitcast.83) | data formatting | bytes 65536 | tf_op jit(solution)/shard_map/reshape | solution.py:513
  16.7 0.0 copy-start.1
  16.7 3.1 %copy.34 = bf16[1,4096,160]{2,1,0:T(8,128)(2,1)S(1)} copy(bf16[1,4096,160]{1,2,0:T(8,128)(2,1)} %param.16) | data formatting | bytes 2621440 | tf_op args[3]
  19.8 1.8 %copy.47 = bf16[512,8,160]{2,0,1:T(8,128)(2,1)} copy(bf16[512,8,160]{2,1,0:T(8,128)(2,1)S(1)} %bitcast.75) | data formatting | bytes 2621440 | tf_op jit(solution)/shard_map/reshape;squeeze | solution.py:467
  21.6 0.0 copy-done
  21.6 1.0 %copy.36 = bf16[1,160,1024]{1,2,0:T(8,128)(2,1)} copy(bf16[1,160,1024]{2,1,0:T(8,128)(2,1)S(1)} %copy-done) | data formatting | bytes 655360 | tf_op args[4]
  22.6 0.1 maximum_bitcast_fusion.1
  22.7 0.6 pad.7.fresh_key_ref
  23.3 0.0 copy-done.1
  23.3 0.6 pad.8.fresh_value_ref
  23.9 0.7 copy_bitcast_fusion.3.query_ref
  24.6 12.9 %weigh.1 = (bf16[16,64,128]{2,1,0:T(8,128)(2,1)}, f32[8,16,128]{2,1,0:T(8,128)}) custom-call(s32[1]{0:T(128)} %copy.50.length_ref, bf16[8,16,128]{2,1,0:T(8,128)(2,1)} %copy_bitcast_fusion.3.query_ref, bf16[8,8,128]{2,1,0:T(8,128)(2,1)} %pad.7.fresh_key_ref, bf16[8,8,128]{2,1,0:T(8,128)(2,1)} %pad.8.fresh_value_ref, bf16[8,512,160]{2,1,0:T(8,128)(2,1)} %bitcast.76, ...), custom_call_target="tpu_custom_call" | custom-call | flops 2684354560 | bytes 8388608 | tf_op jit(solution)/shard_map/weigh/pallas_call | solution.py:476
  37.5 1.5 %copy.38 = f32[8,2,8,128]{3,2,0,1:T(8,128)} copy(f32[8,2,8,128]{3,2,1,0:T(8,128)} %bitcast.82) | data formatting | bytes 131072 | tf_op jit(solution)/shard_map/reshape | solution.py:519
  39.0 0.0 all-to-all-done
  39.0 15.4 %gather_fusion = bf16[2048,1024]{1,0:T(8,128)(2,1)} fusion(bf16[4096,1024]{1,0:T(8,128)(2,1)} %param.18, s32[2048]{0:T(1024)S(1)} %broadcast_clamp_fusion), kind=kCustom, calls=%fused_computation | custom fusion | bytes 8396800 | tf_op jit(solution)/shard_map/gather | solution.py:517
  54.4 28.7 %meet.1 = bf16[128,128]{1,0:T(8,128)(2,1)} custom-call(bf16[16,64,128]{2,1,0:T(8,128)(2,1)} %get-tuple-element.10.wire_ref, f32[128,128]{1,0:T(8,128)} %bitcast.79, bf16[2048,1024]{1,0:T(8,128)(2,1)} %gather_fusion), custom_call_target="tpu_custom_call" | custom-call | tf_op jit(solution)/shard_map/meet/pallas_call | solution.py:522
  83.1 1.4 %reshape.140 = bf16[2,1,8192]{2,0,1:T(2,128)(2,1)} reshape(bf16[128,128]{1,0:T(8,128)(2,1)} %meet.1) | data formatting | bytes 65536 | tf_op jit(solution)/shard_map/reshape | solution.py:537
  (5 shorter events, 0.0 us)
Async XLA Ops:
  4.7 16.9 %copy-start = (bf16[1,160,1024]{2,1,0:T(8,128)(2,1)S(1)}, bf16[1,160,1024]{2,1,0:T(8,128)(2,1)}, u32[]{:S(2)}) copy-start(bf16[1,160,1024]{2,1,0:T(8,128)(2,1)} %param.17) | copy-start | bytes 983044
  5.5 33.5 %all-to-all-start = ((s32[16,1,128]{2,1,0:T(1,128)}), s32[16,1,128]{2,1,0:T(1,128)S(1)}, u32[]{:S(2)}, u32[]{:S(2)}) async-start(s32[16,1,128]{2,1,0:T(1,128)} %copy.41), calls=%async_computation | async-start | bytes 16384 | tf_op jit(solution)/shard_map/all_to_all | solution.py:447
  16.7 6.6 %copy-start.1 = (bf16[2,1,1024]{2,0,1:T(2,128)(2,1)S(1)}, bf16[2,1,1024]{2,0,1:T(2,128)(2,1)}, u32[]{:S(2)}) copy-start(bf16[2,1,1024]{2,0,1:T(2,128)(2,1)} %param.15) | copy-start | bytes 12292

commit v4 on v3

--- a/solution.py
+++ b/solution.py
@@ -299,9 +299,11 @@
             )
             weights = [power / denominator for power in powers]
             fresh_weight = (fresh_power / denominator).astype(jnp.bfloat16)
-            fresh_ref[head] = jnp.dot(
+            fresh_part = jnp.dot(
                 fresh_weight, fresh_value_ref[head], preferred_element_type=jnp.float32
             )
+            for s in range(steps):
+                fresh_ref[s, head] = fresh_part[s * group : (s + 1) * group]
             for s in range(steps):
                 table = jnp.where(place[s : s + 1] == slot_at, 1.0, 0.0).astype(jnp.bfloat16)
                 stacked = jnp.concatenate(
@@ -370,10 +372,11 @@
         return 0
 
     lax.fori_loop(1, holders, greet, 0)
-    for k in range(holders):
+    far_first = sorted(range(1, holders), key=lambda k: abs(2 * k - holders))
+    for k in [0] + far_first:
         tile_copy(k).start()
     pl.semaphore_wait(barrier, holders - 1)
-    for k in range(1, holders):
+    for k in far_first:
         weight_copy(k).start()
 
     same = (
@@ -382,29 +385,35 @@
     )
 
     def partial(weight, k):
-        total = jnp.zeros((rows, HEAD_SIZE), jnp.float32)
         weight = weight.astype(jnp.float32)
-        for j in range(in_block):
-            piece = weight[j * group : (j + 1) * group]
-            spread = jnp.where(same, jnp.concatenate([piece] * (rows // group), 0), 0.0)
-            total = total + jnp.dot(
-                spread.astype(jnp.bfloat16),
-                block_ref[k, :, j * HEAD_SIZE : (j + 1) * HEAD_SIZE],
-                preferred_element_type=jnp.float32,
-            )
-        return total
+        spread = [
+            jnp.where(
+                same, jnp.concatenate([weight[j * group : (j + 1) * group]] * (rows // group), 0), 0.0
+            ).astype(jnp.bfloat16)
+            for j in range(in_block)
+        ]
+        values = [
+            block_ref[k, :, j * HEAD_SIZE : (j + 1) * HEAD_SIZE] for j in range(in_block)
+        ]
+        return jnp.dot(
+            jnp.concatenate(spread, 1),
+            jnp.concatenate(values, 0),
+            preferred_element_type=jnp.float32,
+        )
 
     tile_copy(0).wait()
     own = partial(wire_ref[me], 0) + fresh_ref[...]
 
-    def answer(k, _):
-        tile_copy(k).wait()
-        weight_copy(k).wait_recv()
-        part_ref[k] = partial(got_ref[k], k).astype(jnp.bfloat16)
-        part_copy(k).start()
-        return 0
-
-    lax.fori_loop(1, holders, answer, 0)
+    for at in range(0, holders - 1, 3):
+        trio = far_first[at : at + 3]
+        for k in trio:
+            tile_copy(k).wait()
+            weight_copy(k).wait_recv()
+        parts = [partial(got_ref[k], k).astype(jnp.bfloat16) for k in trio]
+        for k, part in zip(trio, parts):
+            part_ref[k] = part
+        for k in trio:
+            part_copy(k).start()
 
     def collect(k, total):
         part_copy(k).wait_recv()
@@ -491,11 +500,11 @@
         ],
         out_specs=(
             whole(holders, BLOCK_TOKENS * group, slots),
-            whole(heads, steps * group, HEAD_SIZE),
+            whole(steps, heads, group, HEAD_SIZE),
         ),
         out_shape=(
             jax.ShapeDtypeStruct((holders, BLOCK_TOKENS * group, slots), jnp.bfloat16),
-            jax.ShapeDtypeStruct((heads, steps * group, HEAD_SIZE), jnp.float32),
+            jax.ShapeDtypeStruct((steps, heads, group, HEAD_SIZE), jnp.float32),
         ),
         scratch_shapes=[
             pltpu.VMEM((heads * HEAD_SIZE, blocks), jnp.float32),
@@ -516,7 +525,6 @@
     )
     tiles = value_tile_store.at[asked.reshape(-1)].get(mode="promise_in_bounds")
     rows = steps * heads * group
-    fresh = fresh.reshape(heads, steps, group, HEAD_SIZE).transpose(1, 0, 2, 3)
     lines = BLOCK_TOKENS * group
     in_vmem = pl.BlockSpec(memory_space=pltpu.VMEM)
     attended = pl.pallas_call(

time: 85.3 us -> 80 us (0.938)
  Pallas kernels: 44.2 us -> 40.4 us
  local copies, waits for them, and re-layouts: 28.3 us -> 26.8 us
    pallas_call x1, Pallas kernels: 28.7 us -> 24.9 us  [routed_device(): pl.pallas_call(functools.partial(meet_kernel, share), in_specs=[in_vmem,...]
    reshape x1 -> x0, local copies, waits for them, and re-layouts: 1.46 us -> none  [routed_device(): fresh = fresh.reshape(heads, steps, group, HEAD_SIZE).transpose(1, 0, 2, 3)]
  transfers between devices with their start and end apart: 1 -> 1, of which waited for: 0 -> 0; matrix products, arithmetic and copies ran while one was open for 15% -> 14% of each run, Pallas kernels for 15% -> 16%
where the time goes in v4:
time: 80 us; the launch traced here: 79.3 us
  Pallas kernels  40.4 us (50%)
  local copies, waits for them, and re-layouts  26.8 us (34%)
  starting transfers between devices  7.38 us (9%)
  other arithmetic  3.91 us (5%)
    pallas_call x1, Pallas kernels, routed_device(): pl.pallas_call(functools.partial(meet_kernel, share), in_specs=[in_vmem,...  24.9 us
    gather x1, local copies, waits for them, and re-layouts, routed_device(): tiles = value_tile_store.at[asked.reshape(-1)].get(mode='promise_in_bounds')  15.4 us
    pallas_call x1, Pallas kernels, routed_device(): pl.pallas_call(functools.partial(weigh_kernel, share), grid=(BLOCK_TOKENS...  12.9 us
    all_to_all x1, starting transfers between devices, routed_device(): lax.all_to_all(request.reshape(holders, slots), 'store', split_axis=0, co...  7.38 us
    unnamed x7, local copies, waits for them, and re-layouts  4.13 us
    pallas_call x1, Pallas kernels, routed_device(): pl.pallas_call(functools.partial(plan_kernel, share), out_shape=(jax.Shap...  2.57 us
    another operation x1, local copies, waits for them, and re-layouts, routed_device(): left = key_left[0].reshape(blocks, BLOCK_TOKENS, rank).transpose(1, 0, 2)  1.76 us
  transfers between devices with their start and end apart: 1, of which 0 were waited for; matrix products, arithmetic and copies ran while one was open for 14% of the time, Pallas kernels for 16%

profile of v4, /device:TPU:0, one launch (start us, length us, event | category | flops | bytes accessed | tf_op | source)
XLA Modules:
  0.0 79.3 jit_solution(16793217945900282577)
XLA Ops:
  0.0 1.3 %add_select_fusion = (s32[8,512]{1,0:T(8,128)}, s32[8,512]{1,0:T(8,128)}) fusion(s32[1,8,512]{2,1,0:T(8,128)} %param.19), kind=kLoop, calls=%fused_computation.12 | loop fusion | flops 77824 | bytes 49152 | tf_op jit(solution)/shard_map/jit(remainder)/select_n | solution.py:446
  1.3 2.6 %plan.1 = (s32[16,512]{1,0:T(8,128)}, s32[16,128]{1,0:T(8,128)}) custom-call(s32[16,64]{1,0:T(8,128)} %bitcast.82, s32[8,512]{1,0:T(8,128)} %get-tuple-element.16.keeper_ref, s32[8,512]{1,0:T(8,128)} %get-tuple-element.15.inside_ref), custom_call_target="tpu_custom_call" | custom-call | tf_op jit(solution)/shard_map/plan/pallas_call | solution.py:447
  3.9 0.8 %copy.35 = s32[16,128]{0,1:T(8,128)S(1)} copy(s32[16,128]{1,0:T(8,128)} %get-tuple-element.12) | data formatting | bytes 16384 | tf_op jit(solution)/shard_map/plan/pallas_call | solution.py:447
  4.7 0.0 copy-start
  4.7 0.1 copy.36
  4.8 0.7 copy.37
  5.5 7.4 %all-to-all-start = ((s32[16,1,128]{2,1,0:T(1,128)}), s32[16,1,128]{2,1,0:T(1,128)S(1)}, u32[]{:S(2)}, u32[]{:S(2)}) async-start(s32[16,1,128]{2,1,0:T(1,128)} %copy.37), calls=%async_computation | async-start | bytes 16384 | tf_op jit(solution)/shard_map/all_to_all | solution.py:456
  13.6 0.8 convert_bitcast_fusion
  14.4 0.7 bitcast_convert_fusion
  15.1 0.1 multiply_cosine_fusion
  15.2 0.1 fusion
  15.3 0.1 subtract_convert_fusion.1
  15.3 1.4 %copy.45 = s32[2,8,512]{2,0,1:T(2,128)} copy(s32[2,8,512]{2,1,0:T(8,128)} %bitcast.79) | data formatting | bytes 65536 | tf_op jit(solution)/shard_map/reshape | solution.py:522
  16.7 0.0 copy-start.1
  16.7 3.1 %copy.31 = bf16[1,4096,160]{2,1,0:T(8,128)(2,1)S(1)} copy(bf16[1,4096,160]{1,2,0:T(8,128)(2,1)} %param.16) | data formatting | bytes 2621440 | tf_op args[3]
  19.8 1.8 %copy.43 = bf16[512,8,160]{2,0,1:T(8,128)(2,1)} copy(bf16[512,8,160]{2,1,0:T(8,128)(2,1)S(1)} %bitcast.72) | data formatting | bytes 2621440 | tf_op jit(solution)/shard_map/reshape;squeeze | solution.py:476
  21.6 0.0 copy-done
  21.6 1.0 %copy.33 = bf16[1,160,1024]{1,2,0:T(8,128)(2,1)} copy(bf16[1,160,1024]{2,1,0:T(8,128)(2,1)S(1)} %copy-done) | data formatting | bytes 655360 | tf_op args[4]
  22.6 0.1 maximum_bitcast_fusion.1
  22.7 0.6 pad.7.fresh_key_ref
  23.3 0.0 copy-done.1
  23.3 0.6 pad.8.fresh_value_ref
  23.9 0.7 copy_bitcast_fusion.3.query_ref
  24.6 12.9 %weigh.1 = (bf16[16,64,128]{2,1,0:T(8,128)(2,1)}, f32[2,8,8,128]{3,2,1,0:T(8,128)}) custom-call(s32[1]{0:T(128)} %copy.46.length_ref, bf16[8,16,128]{2,1,0:T(8,128)(2,1)} %copy_bitcast_fusion.3.query_ref, bf16[8,8,128]{2,1,0:T(8,128)(2,1)} %pad.7.fresh_key_ref, bf16[8,8,128]{2,1,0:T(8,128)(2,1)} %pad.8.fresh_value_ref, bf16[8,512,160]{2,1,0:T(8,128)(2,1)} %bitcast.73, ...), custom_call_target="tpu_custom_call" | custom-call | flops 2684354560 | bytes 8388608 | tf_op jit(solution)/shard_map/weigh/pallas_call | solution.py:485
  37.5 0.0 all-to-all-done
  37.6 15.4 %gather_fusion = bf16[2048,1024]{1,0:T(8,128)(2,1)} fusion(bf16[4096,1024]{1,0:T(8,128)(2,1)} %param.18, s32[2048]{0:T(1024)S(1)} %broadcast_clamp_fusion), kind=kCustom, calls=%fused_computation | custom fusion | bytes 8396800 | tf_op jit(solution)/shard_map/gather | solution.py:526
  52.9 24.9 %meet.1 = bf16[128,128]{1,0:T(8,128)(2,1)} custom-call(bf16[16,64,128]{2,1,0:T(8,128)(2,1)} %get-tuple-element.10.wire_ref, f32[128,128]{1,0:T(8,128)} %bitcast.78, bf16[2048,1024]{1,0:T(8,128)(2,1)} %gather_fusion), custom_call_target="tpu_custom_call" | custom-call | tf_op jit(solution)/shard_map/meet/pallas_call | solution.py:530
  77.9 1.4 %reshape.136 = bf16[2,1,8192]{2,0,1:T(2,128)(2,1)} reshape(bf16[128,128]{1,0:T(8,128)(2,1)} %meet.1) | data formatting | bytes 65536 | tf_op jit(solution)/shard_map/reshape | solution.py:545
  (5 shorter events, 0.0 us)
Async XLA Ops:
  4.7 16.9 %copy-start = (bf16[1,160,1024]{2,1,0:T(8,128)(2,1)S(1)}, bf16[1,160,1024]{2,1,0:T(8,128)(2,1)}, u32[]{:S(2)}) copy-start(bf16[1,160,1024]{2,1,0:T(8,128)(2,1)} %param.17) | copy-start | bytes 983044
  5.5 32.0 %all-to-all-start = ((s32[16,1,128]{2,1,0:T(1,128)}), s32[16,1,128]{2,1,0:T(1,128)S(1)}, u32[]{:S(2)}, u32[]{:S(2)}) async-start(s32[16,1,128]{2,1,0:T(1,128)} %copy.37), calls=%async_computation | async-start | bytes 16384 | tf_op jit(solution)/shard_map/all_to_all | solution.py:456
  16.7 6.6 %copy-start.1 = (bf16[2,1,1024]{2,0,1:T(2,128)(2,1)S(1)}, bf16[2,1,1024]{2,0,1:T(2,128)(2,1)}, u32[]{:S(2)}) copy-start(bf16[2,1,1024]{2,0,1:T(2,128)(2,1)} %param.15) | copy-start | bytes 12292

commit v5 on v4

--- a/solution.py
+++ b/solution.py
@@ -182,11 +182,26 @@
     return jnp.stack(results)
 
 
-def plan_kernel(share, chosen_ref, keeper_ref, inside_ref, place_ref, request_ref):
+def plan_kernel(
+    share, chosen_ref, keeper_ref, inside_ref, place_ref, asked_ref,
+    send_ref, recv_ref, send_sem, recv_sem,
+):
+    me = lax.axis_index("store")
+    count = asked_ref.shape[0]
+    barrier = pltpu.get_barrier_semaphore()
+
+    def greet(k, _):
+        pl.semaphore_signal(
+            barrier, inc=1, device_id={"store": lax.rem(me + k, count)},
+            device_id_type=pl.DeviceIdType.MESH,
+        )
+        return 0
+
+    lax.fori_loop(1, count, greet, 0)
     rows, picks = chosen_ref.shape
     heads, blocks = keeper_ref.shape
-    total = request_ref.shape[1]
-    holders = total // share
+    holders = count
+    total = holders * share
     block_at = lax.broadcasted_iota(jnp.int32, (rows, blocks), 1)
     chosen = chosen_ref[...]
     hit = jnp.zeros((rows, blocks), jnp.int32)
@@ -212,6 +227,7 @@
     middle = ((inside >> 8) & 255).astype(jnp.float32)
     high = (inside >> 16).astype(jnp.float32)
     slot_at = lax.broadcasted_iota(jnp.int32, (total, blocks), 0)
+    moved = []
     for row in range(rows):
         head = row % heads
         digits = jnp.concatenate(
@@ -222,7 +238,37 @@
         found = lax.dot_general(
             digits, table, (((1,), (1,)), ((), ())), preferred_element_type=jnp.float32
         ).astype(jnp.int32)
-        request_ref[row : row + 1, :] = found[0:1] + found[1:2] * 256 + found[2:3] * 65536
+        found = found[0:1] + found[1:2] * 256 + found[2:3] * 65536
+        moved.append(pltpu.roll(found, row * share, 1) if row else found)
+    moved = jnp.concatenate(moved, 0)
+    own_lanes = (
+        lax.broadcasted_iota(jnp.int32, (rows, total), 1) // share
+        == lax.broadcasted_iota(jnp.int32, (rows, total), 0)
+    )
+    for holder in range(holders):
+        turned = pltpu.roll(moved, total - holder * share, 1) if holder else moved
+        send_ref[holder] = jnp.sum(jnp.where(own_lanes, turned, 0), 0, keepdims=True)
+
+    def copy(k):
+        peer = lax.rem(me + k, holders)
+        return pltpu.make_async_remote_copy(
+            src_ref=send_ref.at[peer],
+            dst_ref=recv_ref.at[k],
+            send_sem=send_sem.at[k],
+            recv_sem=recv_sem.at[k],
+            device_id={"store": peer},
+            device_id_type=pl.DeviceIdType.MESH,
+        )
+
+    pl.semaphore_wait(barrier, holders - 1)
+    for k in range(1, holders):
+        copy(k).start()
+    asked_ref[0] = send_ref[me]
+    for k in range(1, holders):
+        copy(k).wait_recv()
+        asked_ref[k] = recv_ref[k]
+    for k in range(1, holders):
+        copy(k).wait_send()
 
 
 def weigh_kernel(
@@ -333,9 +379,8 @@
     me = lax.axis_index("store")
 
     def tile_copy(k):
-        source = lax.rem(me - k + holders, holders)
         return pltpu.make_async_copy(
-            tiles_ref.at[pl.ds(pl.multiple_of(source * lanes, lanes), lanes)],
+            tiles_ref.at[pl.ds(k * lanes, lanes)],
             block_ref.at[k],
             tile_sem.at[k],
         )
@@ -441,21 +486,23 @@
     group = queries.shape[2] // HEAD_SIZE // heads
     rank = key_left.shape[2]
     slots = steps * heads * share
-    total = holders * share
     keeper = slot_map[0] // pool_here
     inside = slot_map[0] % pool_here
-    place, request = pl.pallas_call(
+    place, asked = pl.pallas_call(
         functools.partial(plan_kernel, share),
         out_shape=(
             jax.ShapeDtypeStruct((steps * heads, blocks), jnp.int32),
-            jax.ShapeDtypeStruct((steps * heads, total), jnp.int32),
+            jax.ShapeDtypeStruct((holders, 1, slots), jnp.int32),
         ),
+        scratch_shapes=[
+            pltpu.VMEM((holders, 1, slots), jnp.int32),
+            pltpu.VMEM((holders, 1, slots), jnp.int32),
+            pltpu.SemaphoreType.DMA((holders,)),
+            pltpu.SemaphoreType.DMA((holders,)),
+        ],
+        compiler_params=pltpu.CompilerParams(collective_id=1, has_side_effects=True),
         name="plan",
     )(chosen[:, 0].reshape(steps * heads, picks), keeper, inside)
-    request = request.reshape(steps * heads, holders, share).transpose(1, 0, 2)
-    asked = lax.all_to_all(
-        request.reshape(holders, slots), "store", split_axis=0, concat_axis=0, tiled=True
-    )
 
     length = lengths[0]
     query = apply_rotary(
@@ -560,7 +607,8 @@
     out_specs = P(None, ("groups", "store"), None)
     def body(*args):
         share = max(1, args[6].shape[2] // mesh.shape["store"] // 4)
-        return (routed_device if share == 8 else per_device)(*args)
+        square = args[7].shape[0] * args[7].shape[2] == mesh.shape["store"]
+        return (routed_device if share == 8 and square else per_device)(*args)
 
     return jax.shard_map(
         body, mesh=mesh, in_specs=in_specs, out_specs=out_specs, check_vma=False

time: 80 us -> 77.9 us (0.974)
  starting transfers between devices: 7.38 us -> 0 us
  Pallas kernels: 40.4 us -> 47.3 us
  local copies, waits for them, and re-layouts: 26.8 us -> 25.3 us
    pallas_call x1, Pallas kernels: 2.57 us -> 10.7 us  [routed_device(): pl.pallas_call(functools.partial(plan_kernel, share), out_shape=(jax.Shap...]
    all_to_all x1 -> x0, starting transfers between devices: 7.38 us -> none  [routed_device(): lax.all_to_all(request.reshape(holders, slots), 'store', split_axis=0, co...]
    pallas_call x1, Pallas kernels: 24.9 us -> 23.6 us  [routed_device(): pl.pallas_call(functools.partial(meet_kernel, share), in_specs=[in_vmem,...]
    unnamed x7 -> x9, local copies, waits for them, and re-layouts: 4.13 us -> 4.14 us
  transfers between devices with their start and end apart: 1 -> 0, of which waited for: 0 -> 0; matrix products, arithmetic and copies ran while one was open for 14% -> 0% of each run, Pallas kernels for 16% -> 0%
where the time goes in v5:
time: 77.9 us; the launch traced here: 77.2 us
  Pallas kernels  47.3 us (61%)
  local copies, waits for them, and re-layouts  25.3 us (32%)
  other arithmetic  3.91 us (5%)
    pallas_call x1, Pallas kernels, routed_device(): pl.pallas_call(functools.partial(meet_kernel, share), in_specs=[in_vmem,...  23.6 us
    gather x1, local copies, waits for them, and re-layouts, routed_device(): tiles = value_tile_store.at[asked.reshape(-1)].get(mode='promise_in_bounds')  15.4 us
    pallas_call x1, Pallas kernels, routed_device(): pl.pallas_call(functools.partial(weigh_kernel, share), grid=(BLOCK_TOKENS...  12.9 us
    pallas_call x1, Pallas kernels, routed_device(): pl.pallas_call(functools.partial(plan_kernel, share), out_shape=(jax.Shap...  10.7 us
    unnamed x9, local copies, waits for them, and re-layouts  4.14 us
    another operation x1, local copies, waits for them, and re-layouts, routed_device(): left = key_left[0].reshape(blocks, BLOCK_TOKENS, rank).transpose(1, 0, 2)  1.76 us

profile of v5, /device:TPU:0, one launch (start us, length us, event | category | flops | bytes accessed | tf_op | source)
XLA Modules:
  0.0 77.2 jit_solution(293523025432751047)
XLA Ops:
  0.7 0.0 copy-start
  0.7 0.1 multiply_cosine_fusion
  0.8 0.8 %convert_bitcast_fusion = f32[1,2,64,128]{3,1,2,0:T(2,128)S(1)} fusion(bf16[2,1,8192]{2,0,1:T(2,128)(2,1)} %param.13), kind=kLoop, calls=%fused_computation.3 | loop fusion | flops 16384 | bytes 98304
  1.6 0.1 fusion
  1.7 0.7 copy_bitcast_fusion.3.query_ref
  2.4 0.7 bitcast_convert_fusion
  3.1 0.1 subtract_convert_fusion.1
  3.2 0.1 maximum_bitcast_fusion.1
  3.3 0.6 pad.7.fresh_key_ref
  3.9 1.3 %add_select_fusion = (s32[8,512]{1,0:T(8,128)}, s32[8,512]{1,0:T(8,128)}) fusion(s32[1,8,512]{2,1,0:T(8,128)} %param.19), kind=kLoop, calls=%fused_computation.12 | loop fusion | flops 77824 | bytes 49152 | tf_op jit(solution)/shard_map/jit(remainder)/select_n | solution.py:490
  5.2 10.7 %plan.1 = (s32[16,512]{1,0:T(8,128)}, s32[16,1,128]{2,1,0:T(1,128)}) custom-call(s32[16,64]{1,0:T(8,128)} %bitcast.76, s32[8,512]{1,0:T(8,128)} %get-tuple-element.16.keeper_ref, s32[8,512]{1,0:T(8,128)} %get-tuple-element.15.inside_ref), custom_call_target="tpu_custom_call" | custom-call | tf_op jit(solution)/shard_map/plan/pallas_call | solution.py:491
  15.9 1.4 %copy.27 = s32[2,8,512]{2,0,1:T(2,128)} copy(s32[2,8,512]{2,1,0:T(8,128)} %bitcast.74) | data formatting | bytes 65536 | tf_op jit(solution)/shard_map/reshape | solution.py:569
  17.3 0.0 copy-start.2
  17.3 3.1 %copy.16 = bf16[1,4096,160]{2,1,0:T(8,128)(2,1)S(1)} copy(bf16[1,4096,160]{1,2,0:T(8,128)(2,1)} %param.16) | data formatting | bytes 2621440 | tf_op args[3]
  20.4 1.8 %copy.25 = bf16[512,8,160]{2,0,1:T(8,128)(2,1)} copy(bf16[512,8,160]{2,1,0:T(8,128)(2,1)S(1)} %bitcast.68) | data formatting | bytes 2621440 | tf_op jit(solution)/shard_map/reshape;squeeze | solution.py:523
  22.2 0.0 copy-done
  22.2 1.0 %copy.18 = bf16[1,160,1024]{1,2,0:T(8,128)(2,1)} copy(bf16[1,160,1024]{2,1,0:T(8,128)(2,1)S(1)} %copy-done) | data formatting | bytes 655360 | tf_op args[4]
  23.2 0.0 copy-done.2
  23.2 0.6 pad.8.fresh_value_ref
  23.8 0.0 copy-start.1
  23.8 12.9 %weigh.1 = (bf16[16,64,128]{2,1,0:T(8,128)(2,1)}, f32[2,8,8,128]{3,2,1,0:T(8,128)}) custom-call(s32[1]{0:T(128)} %copy.28.length_ref, bf16[8,16,128]{2,1,0:T(8,128)(2,1)} %copy_bitcast_fusion.3.query_ref, bf16[8,8,128]{2,1,0:T(8,128)(2,1)} %pad.7.fresh_key_ref, bf16[8,8,128]{2,1,0:T(8,128)(2,1)} %pad.8.fresh_value_ref, bf16[8,512,160]{2,1,0:T(8,128)(2,1)} %bitcast.69, ...), custom_call_target="tpu_custom_call" | custom-call | flops 2684354560 | bytes 8388608 | tf_op jit(solution)/shard_map/weigh/pallas_call | solution.py:532
  36.7 0.0 copy-done.1
  36.8 15.4 %gather_fusion = bf16[2048,1024]{1,0:T(8,128)(2,1)} fusion(bf16[4096,1024]{1,0:T(8,128)(2,1)} %param.18, s32[2048]{0:T(1024)S(1)} %broadcast_clamp_fusion), kind=kCustom, calls=%fused_computation | custom fusion | bytes 8396800 | tf_op jit(solution)/shard_map/gather | solution.py:573
  52.2 23.6 %meet.1 = bf16[128,128]{1,0:T(8,128)(2,1)} custom-call(bf16[16,64,128]{2,1,0:T(8,128)(2,1)} %get-tuple-element.10.wire_ref, f32[128,128]{1,0:T(8,128)} %bitcast.72, bf16[2048,1024]{1,0:T(8,128)(2,1)} %gather_fusion), custom_call_target="tpu_custom_call" | custom-call | tf_op jit(solution)/shard_map/meet/pallas_call | solution.py:577
  75.8 1.4 %reshape.127 = bf16[2,1,8192]{2,0,1:T(2,128)(2,1)} reshape(bf16[128,128]{1,0:T(8,128)(2,1)} %meet.1) | data formatting | bytes 65536 | tf_op jit(solution)/shard_map/reshape | solution.py:592
  (5 shorter events, 0.0 us)
Async XLA Ops:
  0.7 21.5 %copy-start = (bf16[1,160,1024]{2,1,0:T(8,128)(2,1)S(1)}, bf16[1,160,1024]{2,1,0:T(8,128)(2,1)}, u32[]{:S(2)}) copy-start(bf16[1,160,1024]{2,1,0:T(8,128)(2,1)} %param.17) | copy-start | bytes 983044
  17.3 5.9 %copy-start.2 = (bf16[2,1,1024]{2,0,1:T(2,128)(2,1)S(1)}, bf16[2,1,1024]{2,0,1:T(2,128)(2,1)}, u32[]{:S(2)}) copy-start(bf16[2,1,1024]{2,0,1:T(2,128)(2,1)} %param.15) | copy-start | bytes 12292
  23.8 12.9 %copy-start.1 = (s32[16,1,128]{2,1,0:T(1,128)S(1)}, s32[16,1,128]{2,1,0:T(1,128)}, u32[]{:S(2)}) copy-start(s32[16,1,128]{2,1,0:T(1,128)} %get-tuple-element.12) | copy-start | bytes 24580

commit v6 on v5

--- a/solution.py
+++ b/solution.py
@@ -280,7 +280,7 @@
     in_block = pl.num_programs(0)
     heads, both, _ = query_ref.shape
     blocks = left_ref.shape[1]
-    steps = place_ref.shape[1]
+    steps = place_ref.shape[0] // heads
     group = both // steps
     holders = wire_ref.shape[0]
     half = HEAD_SIZE // 2
@@ -315,7 +315,9 @@
 
         def one_head(head, _):
             query = query_ref[head]
-            place = place_ref[head]
+            place = jnp.concatenate(
+                [place_ref[pl.ds(s * heads + head, 1)] for s in range(steps)], 0
+            )
             place_rows = jnp.concatenate(
                 [jnp.broadcast_to(place[s : s + 1], (group, blocks)) for s in range(steps)], 0
             )
@@ -539,7 +541,7 @@
             whole(heads, 8, HEAD_SIZE),
             per_token(blocks, rank),
             whole(heads * HEAD_SIZE, rank),
-            whole(heads, steps, blocks),
+            whole(steps * heads, blocks),
             whole(half, blocks),
             whole(half, blocks),
             per_token(half, 1),
@@ -566,7 +568,7 @@
         name="weigh",
     )(
         lengths, query, fresh_key, fresh_value, left, right_key_factor[0].T,
-        place.reshape(steps, heads, blocks).transpose(1, 0, 2),
+        place,
         constant(np.cos(coarse)), constant(np.sin(coarse)),
         constant(np.cos(fine)), constant(np.sin(fine)),
     )

time: 77.9 us -> 76.5 us (0.982)
  local copies, waits for them, and re-layouts: 25.3 us -> 23.9 us
    reshape x1 -> x0, local copies, waits for them, and re-layouts: 1.4 us -> none  [routed_device(): place.reshape(steps, heads, blocks).transpose(1, 0, 2)]
where the time goes in v6:
time: 76.5 us; the launch traced here: 75.9 us
  Pallas kernels  47.3 us (62%)
  local copies, waits for them, and re-layouts  23.9 us (31%)
  other arithmetic  3.9 us (5%)
  between operations  0.79 us (1%)
    pallas_call x1, Pallas kernels, routed_device(): pl.pallas_call(functools.partial(meet_kernel, share), in_specs=[in_vmem,...  23.6 us
    gather x1, local copies, waits for them, and re-layouts, routed_device(): tiles = value_tile_store.at[asked.reshape(-1)].get(mode='promise_in_bounds')  15.4 us
    pallas_call x1, Pallas kernels, routed_device(): pl.pallas_call(functools.partial(weigh_kernel, share), grid=(BLOCK_TOKENS...  12.9 us
    pallas_call x1, Pallas kernels, routed_device(): pl.pallas_call(functools.partial(plan_kernel, share), out_shape=(jax.Shap...  10.7 us
    unnamed x9, local copies, waits for them, and re-layouts  4.13 us
    another operation x1, local copies, waits for them, and re-layouts, routed_device(): left = key_left[0].reshape(blocks, BLOCK_TOKENS, rank).transpose(1, 0, 2)  1.76 us

profile of v6, /device:TPU:0, one launch (start us, length us, event | category | flops | bytes accessed | tf_op | source)
XLA Modules:
  0.0 75.9 jit_solution(18309504182285561434)
XLA Ops:
  0.0 0.0 copy-start
  0.7 0.1 multiply_cosine_fusion
  0.8 0.8 %convert_bitcast_fusion = f32[1,2,64,128]{3,1,2,0:T(2,128)S(1)} fusion(bf16[2,1,8192]{2,0,1:T(2,128)(2,1)} %param.13), kind=kLoop, calls=%fused_computation.3 | loop fusion | flops 16384 | bytes 98304
  1.6 0.1 fusion
  1.7 0.7 copy_bitcast_fusion.2.query_ref
  2.4 0.7 bitcast_convert_fusion
  3.1 0.1 subtract_convert_fusion.1
  3.2 0.1 maximum_bitcast_fusion.1
  3.3 0.6 pad.7.fresh_key_ref
  3.9 1.3 %add_select_fusion = (s32[8,512]{1,0:T(8,128)}, s32[8,512]{1,0:T(8,128)}) fusion(s32[1,8,512]{2,1,0:T(8,128)} %param.19), kind=kLoop, calls=%fused_computation.11 | loop fusion | flops 77824 | bytes 49152 | tf_op jit(solution)/shard_map/jit(remainder)/select_n | solution.py:492
  5.2 10.7 %plan.1 = (s32[16,512]{1,0:T(8,128)}, s32[16,1,128]{2,1,0:T(1,128)}) custom-call(s32[16,64]{1,0:T(8,128)} %bitcast.70, s32[8,512]{1,0:T(8,128)} %get-tuple-element.16.keeper_ref, s32[8,512]{1,0:T(8,128)} %get-tuple-element.15.inside_ref), custom_call_target="tpu_custom_call" | custom-call | tf_op jit(solution)/shard_map/plan/pallas_call | solution.py:493
  15.9 0.0 copy-start.2
  16.0 3.1 %copy.16 = bf16[1,4096,160]{2,1,0:T(8,128)(2,1)S(1)} copy(bf16[1,4096,160]{1,2,0:T(8,128)(2,1)} %param.16) | data formatting | bytes 2621440 | tf_op args[3]
  19.1 1.8 %copy.23 = bf16[512,8,160]{2,0,1:T(8,128)(2,1)} copy(bf16[512,8,160]{2,1,0:T(8,128)(2,1)S(1)} %bitcast.64) | data formatting | bytes 2621440 | tf_op jit(solution)/shard_map/reshape;squeeze | solution.py:525
  20.8 0.0 copy-done
  20.8 1.0 %copy.18 = bf16[1,160,1024]{1,2,0:T(8,128)(2,1)} copy(bf16[1,160,1024]{2,1,0:T(8,128)(2,1)S(1)} %copy-done) | data formatting | bytes 655360 | tf_op args[4]
  21.8 0.0 copy-done.2
  21.8 0.6 pad.8.fresh_value_ref
  22.4 0.0 copy-start.1
  22.5 12.9 %weigh.1 = (bf16[16,64,128]{2,1,0:T(8,128)(2,1)}, f32[2,8,8,128]{3,2,1,0:T(8,128)}) custom-call(s32[1]{0:T(128)} %copy.25.length_ref, bf16[8,16,128]{2,1,0:T(8,128)(2,1)} %copy_bitcast_fusion.2.query_ref, bf16[8,8,128]{2,1,0:T(8,128)(2,1)} %pad.7.fresh_key_ref, bf16[8,8,128]{2,1,0:T(8,128)(2,1)} %pad.8.fresh_value_ref, bf16[8,512,160]{2,1,0:T(8,128)(2,1)} %bitcast.65, ...), custom_call_target="tpu_custom_call" | custom-call | flops 2684354560 | bytes 8388608 | tf_op jit(solution)/shard_map/weigh/pallas_call | solution.py:534
  35.4 0.0 copy-done.1
  35.4 15.4 %gather_fusion = bf16[2048,1024]{1,0:T(8,128)(2,1)} fusion(bf16[4096,1024]{1,0:T(8,128)(2,1)} %param.18, s32[2048]{0:T(1024)S(1)} %broadcast_clamp_fusion), kind=kCustom, calls=%fused_computation | custom fusion | bytes 8396800 | tf_op jit(solution)/shard_map/gather | solution.py:575
  50.8 23.6 %meet.1 = bf16[128,128]{1,0:T(8,128)(2,1)} custom-call(bf16[16,64,128]{2,1,0:T(8,128)(2,1)} %get-tuple-element.10.wire_ref, f32[128,128]{1,0:T(8,128)} %bitcast.68, bf16[2048,1024]{1,0:T(8,128)(2,1)} %gather_fusion), custom_call_target="tpu_custom_call" | custom-call | tf_op jit(solution)/shard_map/meet/pallas_call | solution.py:579
  74.5 1.4 %reshape.123 = bf16[2,1,8192]{2,0,1:T(2,128)(2,1)} reshape(bf16[128,128]{1,0:T(8,128)(2,1)} %meet.1) | data formatting | bytes 65536 | tf_op jit(solution)/shard_map/reshape | solution.py:594
  (5 shorter events, 0.0 us)
Async XLA Ops:
  0.0 20.8 %copy-start = (bf16[1,160,1024]{2,1,0:T(8,128)(2,1)S(1)}, bf16[1,160,1024]{2,1,0:T(8,128)(2,1)}, u32[]{:S(2)}) copy-start(bf16[1,160,1024]{2,1,0:T(8,128)(2,1)} %param.17) | copy-start | bytes 983044
  15.9 5.9 %copy-start.2 = (bf16[2,1,1024]{2,0,1:T(2,128)(2,1)S(1)}, bf16[2,1,1024]{2,0,1:T(2,128)(2,1)}, u32[]{:S(2)}) copy-start(bf16[2,1,1024]{2,0,1:T(2,128)(2,1)} %param.15) | copy-start | bytes 12292
  22.4 12.9 %copy-start.1 = (s32[16,1,128]{2,1,0:T(1,128)S(1)}, s32[16,1,128]{2,1,0:T(1,128)}, u32[]{:S(2)}) copy-start(s32[16,1,128]{2,1,0:T(1,128)} %get-tuple-element.12) | copy-start | bytes 24580
